TPU v7x, 32 devices: a whole 2x2x4 slice. The times are simulated.
32 devices in a mesh: band: 16 (over z, y, x), mem: 2 (over core).
Axes of the slice: x: 2, y: 2, z: 4, core: 2. Of those that a mesh axis runs over, the one named last changes fastest.
Arguments:
- state: float32 [16384, 2048], P('band', 'mem'), may hold values from -10 to 10
- obs_anom: bfloat16 [4096, 2048], P('band', 'mem'), may hold values from -8 to 8
- innov: float32 [4096, 2048], P('band', 'mem'), may hold values from -12 to 12
- pattern: int32 [16, 4, 8, 4], P('band'), may hold values 0 or 1
- distance: int32 [16, 4, 8, 4], P('band'), may hold values from 0 to 7
- taper: float32 [8], replicated, may hold values from 0.2 to 1
- order: int32 [16, 4], P('band'), may hold values from 0 to 3, each once within a row
Outputs:
- analysis: float32 [16384, 2048], P('band', 'mem')
Inputs may be any that keep to these rules, and one draw needn't show every extreme that they name: Each row of order lists 0 .. 3 once each.
All inputs are finite; a program needn't handle non-finite values. No bound on the sum of `pattern` on one device may be relied on, other than what follows from the above.
Results may differ from a plain program's by a relative error of at most 0.0028.
Values may be sent and summed in bfloat16 or wider, within the bound.
A program may use at most 64 MiB of HBM per device.

v0:
```python
import functools

import jax
import jax.numpy as jnp
from jax import lax
from jax.experimental import pallas as pl
from jax.experimental.pallas import tpu as pltpu
from jax.sharding import PartitionSpec as P


F32 = jnp.float32
BF16 = jnp.bfloat16
VMEM_SPEC = pl.BlockSpec(memory_space=pltpu.VMEM)
SMEM_SPEC = pl.BlockSpec(memory_space=pltpu.SMEM)


def from_behind(value, axis, steps):
    count = lax.axis_size(axis)
    pairs = [(source, (source + steps) % count) for source in range(count)]
    return lax.ppermute(value, axis, pairs)


def member_parts(value):
    if lax.axis_size("mem") == 2:
        return [value, from_behind(value, "mem", 1)]
    return [lax.psum(value, "mem")]


def halves(value):
    high = value.astype(BF16)
    return high, (value - high.astype(F32)).astype(BF16)


def mm(a, b):
    return jnp.dot(a, b, preferred_element_type=F32)


def mm3(a, b):
    a_high, a_low = halves(a)
    b_high, b_low = halves(b)
    return mm(a_high, b_high) + (mm(a_high, b_low) + mm(a_low, b_high))


def mm_full(a, b):
    return jnp.dot(a, b, precision=lax.Precision.HIGHEST, preferred_element_type=F32)


def nt(a, b):
    return lax.dot_general(a, b, (((1,), (1,)), ((), ())), preferred_element_type=F32)


def weigh_kernel(scale, part_count, *refs):
    parts = refs[:part_count]
    d_ref, w_ref, inv = refs[part_count:]
    total = parts[0][...]
    for part in parts[1:]:
        total = total + part[...]
    size = total.shape[0]
    eye = (
        lax.broadcasted_iota(jnp.int32, (size, size), 0)
        == lax.broadcasted_iota(jnp.int32, (size, size), 1)
    ).astype(F32)
    spd = total * scale + eye
    square = mm3(spd, spd)
    bound2 = jnp.max(jnp.sum(jnp.abs(square), axis=1))
    row = jnp.max(jnp.sum(jnp.abs(spd), axis=1))
    top = jnp.minimum(row, jnp.sqrt(bound2 * 1.01)) * 1.001
    ratio = (top - 1.0) / (top + 1.0)
    alpha = 2.0 / (top + 1.0)
    gain = 2.0 / (2.0 - ratio * ratio)
    c0 = 2.0 * alpha * gain
    c1 = -alpha * alpha * gain
    ratio = ratio * ratio * 0.5 * gain
    inv[...] = c0 * eye + c1 * spd
    small = top < 40.0

    def run(product, active):
        def going(ratio):
            return jnp.logical_and(active, ratio > 2e-5)

        def step(ratio):
            now = inv[...]
            gain = 2.0 / (2.0 - ratio * ratio)
            inv[...] = gain * (2.0 * now - product(now, product(spd, now)))
            return ratio * ratio * 0.5 * gain

        lax.while_loop(going, step, ratio)

    run(mm3, small)
    run(mm_full, jnp.logical_not(small))

    @pl.when(small)
    def _():
        w_ref[...] = mm3(inv[...], d_ref[...]).astype(BF16)

    @pl.when(jnp.logical_not(small))
    def _():
        now = inv[...]
        first = mm_full(now, d_ref[...])
        left = d_ref[...] - mm_full(spd, first)
        w_ref[...] = (first + mm_full(now, left)).astype(BF16)


def grouped(group, bands):
    return bands % group == 0 and bands > group and group & (group - 1) == 0


def gathered(value, group):
    bands = lax.axis_size("band")
    if not grouped(group, bands):
        return [value] + [from_behind(value, "band", a) for a in range(1, group)]
    prior = from_behind(value, "band", group)
    place = lax.axis_index("band") % group
    found = [value]
    for flip in range(1, group):
        upward = (place ^ flip) > place
        sent = jnp.where(upward, value, prior)
        found.append(lax.ppermute(sent, "band", [(b, b ^ flip) for b in range(bands)]))
    return found


def slots_of(order, group):
    offset = order[0]
    if not grouped(group, lax.axis_size("band")):
        return offset
    place = lax.axis_index("band") % group
    return (place ^ ((place - offset + group) % group)).astype(jnp.int32)


def pick(slots_ref, arrays, target):
    for step in range(target.shape[0]):
        for slot, array in enumerate(arrays):

            @pl.when(slots_ref[step] == slot)
            def _():
                target[step] = array[...]


def cross_kernel(*refs):
    slots_ref, x_ref = refs[:2]
    arrays = refs[2:-2]
    cross_ref, y_ref = refs[-2:]

    @pl.when(pl.program_id(0) == 0)
    def _():
        pick(slots_ref, arrays, y_ref)

    high = x_ref[...].astype(BF16)
    for step in range(y_ref.shape[0]):
        cross_ref[step] = nt(high, y_ref[step])


def block_weight(tables, step, block, cols):
    order_ref, pattern_ref, distance_ref, taper_ref = tables
    q_count = pattern_ref.shape[3]
    width = cols // q_count
    lane = lax.broadcasted_iota(jnp.int32, (1, cols), 1)
    offset = order_ref[0, step]
    weight = jnp.zeros((1, cols), F32)
    for q in range(q_count):
        value = pattern_ref[0, offset, block, q].astype(F32) * taper_ref[
            distance_ref[0, offset, block, q]
        ]
        weight = jnp.where((lane >= q * width) & (lane < (q + 1) * width), value, weight)
    return weight


def link_kernel(*refs):
    slots_ref, y_ref = refs[:2]
    arrays = refs[2:-2]
    g_ref, w_ref = refs[-2:]
    pick(slots_ref, arrays, w_ref)
    place = 0
    for step in range(1, y_ref.shape[0]):
        for before in range(step):
            g_ref[place] = nt(w_ref[before], y_ref[step])
            place += 1


def apply_kernel(scale, per, part_count, *refs):
    tables = refs[:4]
    crosses = refs[4 : 4 + part_count]
    links = refs[4 + part_count : -5]
    w_ref, x_ref, out_ref, link_high, link_low = refs[-5:]
    count, rows, cols = crosses[0].shape

    @pl.when(pl.program_id(0) == 0)
    def _():
        total = links[0][...]
        for part in links[1:]:
            total = total + part[...]
        link_high[...], link_low[...] = halves(total)

    applied = []
    field = x_ref[...]
    place = 0
    for step in range(count):
        total = crosses[0][step]
        for part in crosses[1:]:
            total = total + part[step]
        for high, low in applied:
            total = total + (
                mm(high, link_high[place]) + (mm(high, link_low[place]) + mm(low, link_high[place]))
            )
            place += 1
        weight = jnp.concatenate(
            [
                jnp.broadcast_to(
                    block_weight(tables, step, pl.program_id(0) * per + r, cols), (rows // per, cols)
                )
                for r in range(per)
            ],
            axis=0,
        )
        change = total * scale * weight
        applied.append(halves(change))
        high, low = applied[-1]
        field = field + (mm(high, w_ref[step]) + mm(low, w_ref[step]))
    out_ref[...] = field


def on_device(state, obs_anom, innov, pattern, distance, taper, order):
    cells, own_members = state.shape
    members = lax.axis_size("mem") * own_members
    scale = 1.0 / (members - 1)
    num_obs = obs_anom.shape[0]
    arrivals = order.shape[1]
    row_blocks = pattern.shape[2]
    rows = cells // row_blocks
    per = 2 if row_blocks % 2 == 0 else 1
    slots = slots_of(order, arrivals)
    gram_parts = member_parts(nt(obs_anom, obs_anom))
    ys = gathered(obs_anom, arrivals)
    solve = pl.pallas_call(
        functools.partial(weigh_kernel, scale, len(gram_parts)),
        out_shape=jax.ShapeDtypeStruct(innov.shape, BF16),
        in_specs=[VMEM_SPEC] * (len(gram_parts) + 1),
        out_specs=VMEM_SPEC,
        scratch_shapes=[pltpu.VMEM((num_obs, num_obs), F32)],
        cost_estimate=pl.CostEstimate(
            flops=60 * num_obs**3, bytes_accessed=8 * innov.size, transcendentals=0
        ),
    )
    weights = solve(*gram_parts, innov)
    slots, weights = lax.optimization_barrier((slots, weights))
    ws = gathered(weights, arrivals)
    tall = per * rows
    row_spec = pl.BlockSpec((arrivals, tall, num_obs), lambda i: (0, i, 0))
    field_spec = pl.BlockSpec((tall, own_members), lambda i: (i, 0))
    batch_shape = (arrivals,) + obs_anom.shape
    batch_spec = pl.BlockSpec(batch_shape, lambda i: (0, 0, 0))
    cross_shape = jax.ShapeDtypeStruct((arrivals, cells, num_obs), F32)
    cross_call = pl.pallas_call(
        cross_kernel,
        out_shape=(cross_shape, jax.ShapeDtypeStruct(batch_shape, BF16)),
        grid=(row_blocks // per,),
        in_specs=[SMEM_SPEC, field_spec]
        + [pl.BlockSpec(obs_anom.shape, lambda i: (0, 0))] * len(ys),
        out_specs=(row_spec, batch_spec),
        cost_estimate=pl.CostEstimate(
            flops=2 * arrivals * state.size * num_obs, bytes_accessed=12 * state.size, transcendentals=0
        ),
    )
    cross, y_sorted = cross_call(slots, state, *ys)
    crosses = member_parts(cross)
    tables = (order, pattern, distance, taper)
    ws, cross = lax.optimization_barrier((ws, crosses[0]))
    crosses = [cross] + crosses[1:]
    pairs = arrivals * (arrivals - 1) // 2
    link_shape = (pairs, num_obs, num_obs)
    link, w_sorted = pl.pallas_call(
        link_kernel,
        out_shape=(
            jax.ShapeDtypeStruct(link_shape, F32),
            jax.ShapeDtypeStruct(batch_shape, BF16),
        ),
        in_specs=[SMEM_SPEC] + [VMEM_SPEC] * (1 + len(ws)),
        out_specs=(VMEM_SPEC, VMEM_SPEC),
    )(slots, y_sorted, *ws)
    links = member_parts(link)
    return pl.pallas_call(
        functools.partial(apply_kernel, scale, per, len(crosses)),
        out_shape=jax.ShapeDtypeStruct(state.shape, F32),
        grid=(row_blocks // per,),
        in_specs=[SMEM_SPEC] * 4
        + [row_spec] * len(crosses)
        + [pl.BlockSpec(link_shape, lambda i: (0, 0, 0))] * len(links)
        + [batch_spec, field_spec],
        out_specs=field_spec,
        scratch_shapes=[pltpu.VMEM(link_shape, BF16), pltpu.VMEM(link_shape, BF16)],
    )(*tables, *crosses, *links, w_sorted, state)


def solution(mesh):
    return jax.shard_map(
        on_device,
        mesh=mesh,
        in_specs=(
            P("band", "mem"),
            P("band", "mem"),
            P("band", "mem"),
            P("band", None, None, None),
            P("band", None, None, None),
            P(),
            P("band", None),
        ),
        out_specs=P("band", "mem"),
        check_vma=False,
    )
```

profile of v0, /device:TPU:0, one launch (start us, length us, event | category | flops | bytes accessed | tf_op | source)
XLA Modules:
  0.0 120.1 jit_solution(6632613461325692737)
XLA Ops:
  0.0 3.1 %collective-permute-start.5 = (bf16[256,1024]{1,0:T(8,128)(2,1)}, bf16[256,1024]{1,0:T(8,128)(2,1)S(1)}, u32[]{:S(2)}, u32[]{:S(2)}) collective-permute-start(bf16[256,1024]{1,0:T(8,128)(2,1)} %refs_2_.4), channel_id=1, source_target_pairs={{0,8},{2,10},{4,12},{6,14},{8,16},{10,18},{12,20},{14,22},{16,24},... | collective-permute-start | bytes 1572872 | tf_op jit(solution)/shard_map/ppermute | solution.py:20
  3.1 14.2 %collective-permute-done.5 = bf16[256,1024]{1,0:T(8,128)(2,1)S(1)} collective-permute-done((bf16[256,1024]{1,0:T(8,128)(2,1)}, bf16[256,1024]{1,0:T(8,128)(2,1)S(1)}, u32[]{:S(2)}, u32[]{:S(2)}) %collective-permute-start.5) | collective-permute-done | bytes 524320 | tf_op jit(solution)/shard_map/ppermute | solution.py:20
  17.2 1.1 broadcast_select_fusion
  18.4 2.5 %collective-permute-start.8 = (bf16[256,1024]{1,0:T(8,128)(2,1)S(1)}, bf16[256,1024]{1,0:T(8,128)(2,1)S(1)}, u32[]{:S(2)}, u32[]{:S(2)}) collective-permute-start(bf16[256,1024]{1,0:T(8,128)(2,1)S(1)} %get-tuple-element.27), channel_id=1, source_target_pairs={{0,6},{2,4},{4,2},{6,0},{8,14},{10,12},{12,10},{14,8},{16,22},{18,... | collective-permute-start | bytes 1572872 | tf_op jit(solution)/shard_map/ppermute | solution.py:118
  20.9 0.5 collective-permute-start.7
  21.4 0.5 collective-permute-start.6
  21.9 1.5 %fusion.2.refs_0_ = f32[256,256]{1,0:T(8,128)S(1)} fusion(bf16[256,1024]{1,0:T(8,128)(2,1)} %refs_2_.4), kind=kOutput, calls=%fused_computation.11 | convolution fusion | flops 134217728 | bytes 786432 | tf_op jit(solution)/shard_map/dot_general | solution.py:49
  23.5 0.0 copy-start.5
  23.5 0.1 collective-permute-start
  23.5 1.2 %fusion.refs_0_ = s32[4]{0:T(128)} fusion(s32[1,4]{1,0:T(1,128)} %refs_0_.1, s32[]{:T(128)S(6)} %select_n.49), kind=kLoop, calls=%fused_computation.9 | loop fusion | flops 56 | bytes 36 | tf_op jit(solution)/shard_map/xor | solution.py:127
  24.8 0.3 collective-permute-done.refs_1_
  25.1 0.0 copy-done.5
  25.1 0.0 copy-start.10
  25.1 0.7 copy-done.10
  25.8 6.2 %shard_map.73.refs_2_ = bf16[256,1024]{1,0:T(8,128)(2,1)} custom-call(f32[256,256]{1,0:T(8,128)} %copy-done.5, f32[256,256]{1,0:T(8,128)} %copy-done.10, f32[256,1024]{1,0:T(8,128)} %refs_2_.3), custom_call_target="tpu_custom_call" | custom-call | flops 1006632960 | bytes 2097152 | tf_op jit(solution)/shard_map/pallas_call | solution.py:244
  32.0 0.0 copy-start
  32.0 2.2 %collective-permute-done.8.refs_5_ = bf16[256,1024]{1,0:T(8,128)(2,1)S(1)} collective-permute-done((bf16[256,1024]{1,0:T(8,128)(2,1)S(1)}, bf16[256,1024]{1,0:T(8,128)(2,1)S(1)}, u32[]{:S(2)}, u32[]{:S(2)}) %collective-permute-start.8) | collective-permute-done | bytes 524320 | tf_op jit(solution)/shard_map/ppermute | solution.py:118
  34.2 0.0 copy-start.8
  34.2 9.5 %collective-permute-done.7.refs_4_ = bf16[256,1024]{1,0:T(8,128)(2,1)S(1)} collective-permute-done((bf16[256,1024]{1,0:T(8,128)(2,1)S(1)}, bf16[256,1024]{1,0:T(8,128)(2,1)S(1)}, u32[]{:S(2)}, u32[]{:S(2)}) %collective-permute-start.7) | collective-permute-done | bytes 524320 | tf_op jit(solution)/shard_map/ppermute | solution.py:118
  43.6 0.0 copy-start.9
  43.6 0.0 collective-permute-done.6.refs_3_
  43.7 0.0 copy-done.8
  43.7 0.8 copy-done.9
  44.4 7.7 %shard_map.74 = (f32[4,1024,256]{2,1,0:T(8,128)}, bf16[4,256,1024]{2,1,0:T(8,128)(2,1)}) custom-call(s32[4]{0:T(128)} %fusion.refs_0_, f32[1024,1024]{1,0:T(8,128)} %refs_9_.1, bf16[256,1024]{1,0:T(8,128)(2,1)} %refs_2_.4, bf16[256,1024]{1,0:T(8,128)(2,1)} %collective-permute-done.6.refs_3_, bf16[256,1024]{1,0:T(8,128)(2,1)} %copy-done.9, ...), custom_call_target="tpu_custom_call" | custom-call | flops 2147483648 | bytes 12582912 | tf_op jit(solution)/shard_map/pallas_call | solution.py:264
  52.2 0.0 copy-start.6
  52.2 0.0 copy-start.7
  52.2 0.2 collective-permute-start.9
  52.4 0.0 copy-done
  52.4 0.0 collective-permute-start.1
  52.4 16.0 %collective-permute-done.1 = bf16[256,1024]{1,0:T(8,128)(2,1)S(1)} collective-permute-done((bf16[256,1024]{1,0:T(8,128)(2,1)S(1)}, bf16[256,1024]{1,0:T(8,128)(2,1)S(1)}, u32[]{:S(2)}, u32[]{:S(2)}) %collective-permute-start.1) | collective-permute-done | bytes 524320 | tf_op jit(solution)/shard_map/ppermute | solution.py:20
  68.4 0.1 broadcast_select_fusion.1
  68.5 1.8 %collective-permute-start.4 = (bf16[256,1024]{1,0:T(8,128)(2,1)S(1)}, bf16[256,1024]{1,0:T(8,128)(2,1)S(1)}, u32[]{:S(2)}, u32[]{:S(2)}) collective-permute-start(bf16[256,1024]{1,0:T(8,128)(2,1)S(1)} %get-tuple-element.30), channel_id=1, source_target_pairs={{0,6},{2,4},{4,2},{6,0},{8,14},{10,12},{12,10},{14,8},{16,22},{18,... | collective-permute-start | bytes 1572872 | tf_op jit(solution)/shard_map/ppermute | solution.py:118
  70.3 1.0 collective-permute-start.3
  71.3 0.8 collective-permute-start.2
  72.1 12.2 %collective-permute-done.4.refs_5_ = bf16[256,1024]{1,0:T(8,128)(2,1)S(1)} collective-permute-done((bf16[256,1024]{1,0:T(8,128)(2,1)S(1)}, bf16[256,1024]{1,0:T(8,128)(2,1)S(1)}, u32[]{:S(2)}, u32[]{:S(2)}) %collective-permute-start.4) | collective-permute-done | bytes 524320 | tf_op jit(solution)/shard_map/ppermute | solution.py:118
  84.3 0.0 copy-start.2
  84.3 9.8 %collective-permute-done.3.refs_4_ = bf16[256,1024]{1,0:T(8,128)(2,1)S(1)} collective-permute-done((bf16[256,1024]{1,0:T(8,128)(2,1)S(1)}, bf16[256,1024]{1,0:T(8,128)(2,1)S(1)}, u32[]{:S(2)}, u32[]{:S(2)}) %collective-permute-start.3) | collective-permute-done | bytes 524320 | tf_op jit(solution)/shard_map/ppermute | solution.py:118
  94.1 0.0 copy-start.3
  94.1 0.0 collective-permute-done.2.refs_3_
  94.1 0.0 copy-start.4
  94.1 0.0 copy-done.2
  94.1 0.8 copy-done.3
  94.9 0.2 copy-done.4
  95.1 4.5 %shard_map.75 = (f32[6,256,256]{2,1,0:T(8,128)}, bf16[4,256,1024]{2,1,0:T(8,128)(2,1)}) custom-call(s32[4]{0:T(128)} %fusion.refs_0_, bf16[4,256,1024]{2,1,0:T(8,128)(2,1)} %get-tuple-element.20.refs_1_, bf16[256,1024]{1,0:T(8,128)(2,1)} %shard_map.73.refs_2_, bf16[256,1024]{1,0:T(8,128)(2,1)} %copy-done.4, bf16[256,1024]{1,0:T(8,128)(2,1)} %copy-done.3, ...), custom_call_target="tpu_custom_call" | custom-call | tf_op jit(solution)/shard_map/pallas_call | solution.py:271
  99.7 0.0 collective-permute-start.10
  99.7 0.0 copy-done.6
  99.7 0.7 copy.8.refs_1_
  100.4 0.0 copy-done.7
  100.4 0.7 copy.9.refs_2_
  101.1 2.2 %collective-permute-done.10.refs_7_ = f32[6,256,256]{2,1,0:T(8,128)S(1)} collective-permute-done((f32[6,256,256]{2,1,0:T(8,128)}, f32[6,256,256]{2,1,0:T(8,128)S(1)}, u32[]{:S(2)}, u32[]{:S(2)}) %collective-permute-start.10) | collective-permute-done | bytes 1572896 | tf_op jit(solution)/shard_map/ppermute | solution.py:20
  103.3 0.0 copy-start.1
  103.3 0.0 collective-permute-done.9.refs_5_
  103.3 1.2 %copy-done.1 = f32[6,256,256]{2,1,0:T(8,128)} copy-done((f32[6,256,256]{2,1,0:T(8,128)}, f32[6,256,256]{2,1,0:T(8,128)S(1)}, u32[]{:S(2)}) %copy-start.1) | copy-done | bytes 1572888
  104.5 15.6 %shard_map.76 = f32[1024,1024]{1,0:T(8,128)} custom-call(s32[1,4]{1,0:T(1,128)} %refs_0_.1, s32[1,4,8,4]{3,2,1,0:T(8,128)} %copy.8.refs_1_, s32[1,4,8,4]{3,2,1,0:T(8,128)} %copy.9.refs_2_, f32[8]{0:T(128)} %refs_3_.1, f32[4,1024,256]{2,1,0:T(8,128)} %get-tuple-element.19.refs_4_, f32[4,1024,256]{2,1,0:T(8,128)} %collective-permute-done.9.refs_5_, ...), custom_call_target="tpu_custom_call" | custom-call | tf_op jit(solution)/shard_map/pallas_call | solution.py:281
Async XLA Ops:
  0.0 17.2 %collective-permute-start.5 = (bf16[256,1024]{1,0:T(8,128)(2,1)}, bf16[256,1024]{1,0:T(8,128)(2,1)S(1)}, u32[]{:S(2)}, u32[]{:S(2)}) collective-permute-start(bf16[256,1024]{1,0:T(8,128)(2,1)} %refs_2_.4), channel_id=1, source_target_pairs={{0,8},{2,10},{4,12},{6,14},{8,16},{10,18},{12,20},{14,22},{16,24},... | collective-permute-start | bytes 1572872 | tf_op jit(solution)/shard_map/ppermute | solution.py:20
  18.4 15.8 %collective-permute-start.8 = (bf16[256,1024]{1,0:T(8,128)(2,1)S(1)}, bf16[256,1024]{1,0:T(8,128)(2,1)S(1)}, u32[]{:S(2)}, u32[]{:S(2)}) collective-permute-start(bf16[256,1024]{1,0:T(8,128)(2,1)S(1)} %get-tuple-element.27), channel_id=1, source_target_pairs={{0,6},{2,4},{4,2},{6,0},{8,14},{10,12},{12,10},{14,8},{16,22},{18,... | collective-permute-start | bytes 1572872 | tf_op jit(solution)/shard_map/ppermute | solution.py:118
  20.9 22.8 %collective-permute-start.7 = (bf16[256,1024]{1,0:T(8,128)(2,1)S(1)}, bf16[256,1024]{1,0:T(8,128)(2,1)S(1)}, u32[]{:S(2)}, u32[]{:S(2)}) collective-permute-start(bf16[256,1024]{1,0:T(8,128)(2,1)S(1)} %get-tuple-element.28), channel_id=1, source_target_pairs={{0,4},{2,6},{4,0},{6,2},{8,12},{10,14},{12,8},{14,10},{16,20},{18,... | collective-permute-start | bytes 1572872 | tf_op jit(solution)/shard_map/ppermute | solution.py:118
  21.4 22.3 %collective-permute-start.6 = (bf16[256,1024]{1,0:T(8,128)(2,1)S(1)}, bf16[256,1024]{1,0:T(8,128)(2,1)}, u32[]{:S(2)}, u32[]{:S(2)}) collective-permute-start(bf16[256,1024]{1,0:T(8,128)(2,1)S(1)} %get-tuple-element.29), channel_id=1, source_target_pairs={{0,2},{2,0},{4,6},{6,4},{8,10},{10,8},{12,14},{14,12},{16,18},{18,... | collective-permute-start | bytes 1572872 | tf_op jit(solution)/shard_map/ppermute | solution.py:118
  23.5 1.6 %copy-start.5 = (f32[256,256]{1,0:T(8,128)}, f32[256,256]{1,0:T(8,128)S(1)}, u32[]{:S(2)}) copy-start(f32[256,256]{1,0:T(8,128)S(1)} %fusion.2.refs_0_) | copy-start | bytes 786436
  23.5 1.6 %collective-permute-start = (f32[256,256]{1,0:T(8,128)S(1)}, f32[256,256]{1,0:T(8,128)S(1)}, u32[]{:S(2)}, u32[]{:S(2)}) collective-permute-start(f32[256,256]{1,0:T(8,128)S(1)} %fusion.2.refs_0_), channel_id=1, source_target_pairs={{0,1},{1,0},{2,3},{3,2},{4,5},{5,4},{6,7},{7,6},{8,9},{9,8},{10,11... | collective-permute-start | bytes 786440 | tf_op jit(solution)/shard_map/ppermute | solution.py:20
  25.1 0.7 copy-start.10
  32.0 20.4 %copy-start = (bf16[256,1024]{1,0:T(8,128)(2,1)S(1)}, bf16[256,1024]{1,0:T(8,128)(2,1)}, u32[]{:S(2)}) copy-start(bf16[256,1024]{1,0:T(8,128)(2,1)} %shard_map.73.refs_2_) | copy-start | bytes 1572868
  34.2 9.5 %copy-start.8 = (bf16[256,1024]{1,0:T(8,128)(2,1)}, bf16[256,1024]{1,0:T(8,128)(2,1)S(1)}, u32[]{:S(2)}) copy-start(bf16[256,1024]{1,0:T(8,128)(2,1)S(1)} %collective-permute-done.8.refs_5_) | copy-start | bytes 1572868
  43.6 0.8 copy-start.9
  52.2 47.5 %copy-start.6 = (s32[1,4,8,4]{2,3,1,0:T(4,128)S(1)}, s32[1,4,8,4]{2,3,1,0:T(4,128)}, u32[]{:S(2)}) copy-start(s32[1,4,8,4]{2,3,1,0:T(4,128)} %param.10) | copy-start | bytes 1540
  52.2 48.2 %copy-start.7 = (s32[1,4,8,4]{2,3,1,0:T(4,128)S(1)}, s32[1,4,8,4]{2,3,1,0:T(4,128)}, u32[]{:S(2)}) copy-start(s32[1,4,8,4]{2,3,1,0:T(4,128)} %param.11) | copy-start | bytes 1540
  52.2 51.1 %collective-permute-start.9 = (f32[4,1024,256]{2,1,0:T(8,128)}, f32[4,1024,256]{2,1,0:T(8,128)}, u32[]{:S(2)}, u32[]{:S(2)}) collective-permute-start(f32[4,1024,256]{2,1,0:T(8,128)} %get-tuple-element.19.refs_4_), channel_id=1, source_target_pairs={{0,1},{1,0},{2,3},{3,2},{4,5},{5,4},{6,7},{7,6},{8,9},{9,8},{10,11... | collective-permute-start | bytes 12582920 | tf_op jit(solution)/shard_map/ppermute | solution.py:20
  52.4 16.0 %collective-permute-start.1 = (bf16[256,1024]{1,0:T(8,128)(2,1)S(1)}, bf16[256,1024]{1,0:T(8,128)(2,1)S(1)}, u32[]{:S(2)}, u32[]{:S(2)}) collective-permute-start(bf16[256,1024]{1,0:T(8,128)(2,1)S(1)} %copy-done), channel_id=1, source_target_pairs={{0,8},{2,10},{4,12},{6,14},{8,16},{10,18},{12,20},{14,22},{16,24},... | collective-permute-start | bytes 1572872 | tf_op jit(solution)/shard_map/ppermute | solution.py:20
  68.5 15.8 %collective-permute-start.4 = (bf16[256,1024]{1,0:T(8,128)(2,1)S(1)}, bf16[256,1024]{1,0:T(8,128)(2,1)S(1)}, u32[]{:S(2)}, u32[]{:S(2)}) collective-permute-start(bf16[256,1024]{1,0:T(8,128)(2,1)S(1)} %get-tuple-element.30), channel_id=1, source_target_pairs={{0,6},{2,4},{4,2},{6,0},{8,14},{10,12},{12,10},{14,8},{16,22},{18,... | collective-permute-start | bytes 1572872 | tf_op jit(solution)/shard_map/ppermute | solution.py:118
  70.3 23.8 %collective-permute-start.3 = (bf16[256,1024]{1,0:T(8,128)(2,1)S(1)}, bf16[256,1024]{1,0:T(8,128)(2,1)S(1)}, u32[]{:S(2)}, u32[]{:S(2)}) collective-permute-start(bf16[256,1024]{1,0:T(8,128)(2,1)S(1)} %get-tuple-element.31), channel_id=1, source_target_pairs={{0,4},{2,6},{4,0},{6,2},{8,12},{10,14},{12,8},{14,10},{16,20},{18,... | collective-permute-start | bytes 1572872 | tf_op jit(solution)/shard_map/ppermute | solution.py:118
  71.3 22.8 %collective-permute-start.2 = (bf16[256,1024]{1,0:T(8,128)(2,1)S(1)}, bf16[256,1024]{1,0:T(8,128)(2,1)S(1)}, u32[]{:S(2)}, u32[]{:S(2)}) collective-permute-start(bf16[256,1024]{1,0:T(8,128)(2,1)S(1)} %get-tuple-element.32), channel_id=1, source_target_pairs={{0,2},{2,0},{4,6},{6,4},{8,10},{10,8},{12,14},{14,12},{16,18},{18,... | collective-permute-start | bytes 1572872 | tf_op jit(solution)/shard_map/ppermute | solution.py:118
  84.3 9.8 %copy-start.2 = (bf16[256,1024]{1,0:T(8,128)(2,1)}, bf16[256,1024]{1,0:T(8,128)(2,1)S(1)}, u32[]{:S(2)}) copy-start(bf16[256,1024]{1,0:T(8,128)(2,1)S(1)} %collective-permute-done.4.refs_5_) | copy-start | bytes 1572868
  94.1 0.8 copy-start.3
  94.1 1.0 copy-start.4
  99.7 3.6 %collective-permute-start.10 = (f32[6,256,256]{2,1,0:T(8,128)}, f32[6,256,256]{2,1,0:T(8,128)S(1)}, u32[]{:S(2)}, u32[]{:S(2)}) collective-permute-start(f32[6,256,256]{2,1,0:T(8,128)} %get-tuple-element.25.refs_6_), channel_id=1, source_target_pairs={{0,1},{1,0},{2,3},{3,2},{4,5},{5,4},{6,7},{7,6},{8,9},{9,8},{10,11... | collective-permute-start | bytes 4718600 | tf_op jit(solution)/shard_map/ppermute | solution.py:20
  103.3 1.2 %copy-start.1 = (f32[6,256,256]{2,1,0:T(8,128)}, f32[6,256,256]{2,1,0:T(8,128)S(1)}, u32[]{:S(2)}) copy-start(f32[6,256,256]{2,1,0:T(8,128)S(1)} %collective-permute-done.10.refs_7_) | copy-start | bytes 4718596
where the time goes:
time: 120 us
  waiting for transfers between devices  66.4 us (55%)
  Pallas kernels  34 us (28%)
  starting transfers between devices  10.4 us (9%)
  local copies, waits for them, and re-layouts  5.17 us (4%)
  other arithmetic  2.48 us (2%)
  matrix products  1.54 us (1%)
    ppermute x6, waiting for transfers between devices, gathered(): lax.ppermute(sent, 'band', [(b, b ^ flip) for b in range(bands)])  33.7 us
    ppermute x5, waiting for transfers between devices, from_behind(): return lax.ppermute(value, axis, pairs)  32.7 us
    pallas_call x1, Pallas kernels, on_device(): pl.pallas_call(functools.partial(apply_kernel, scale, per, len(crosses)),...  15.6 us
    pallas_call x1, Pallas kernels, on_device(): cross, y_sorted = cross_call(slots, state, *ys)  7.72 us
    ppermute x6, starting transfers between devices, gathered(): lax.ppermute(sent, 'band', [(b, b ^ flip) for b in range(bands)])  7.11 us
    pallas_call x1, Pallas kernels, on_device(): weights = solve(*gram_parts, innov)  6.18 us
    unnamed x24, local copies, waits for them, and re-layouts  5.17 us
    pallas_call x1, Pallas kernels, on_device(): pl.pallas_call(link_kernel, out_shape=(jax.ShapeDtypeStruct(link_shape, F...  4.54 us
  transfers between devices with their start and end apart: 11, of which 8 were waited for; matrix products, arithmetic and copies ran while one was open for 4% of the time, Pallas kernels for 9%

commit v1 on v0

--- a/solution.py
+++ b/solution.py
@@ -105,16 +105,21 @@
     return bands % group == 0 and bands > group and group & (group - 1) == 0
 
 
-def gathered(value, group):
+def gathered(value, group, tie=None, early=None):
     bands = lax.axis_size("band")
     if not grouped(group, bands):
         return [value] + [from_behind(value, "band", a) for a in range(1, group)]
     prior = from_behind(value, "band", group)
+    if tie is not None:
+        _, prior = lax.optimization_barrier((tie, prior))
     place = lax.axis_index("band") % group
     found = [value]
-    for flip in range(1, group):
-        upward = (place ^ flip) > place
-        sent = jnp.where(upward, value, prior)
+    sends = [
+        jnp.where((place ^ flip) > place, value, prior) for flip in range(1, group)
+    ]
+    if early is not None:
+        sends, early[0] = lax.optimization_barrier((sends, early[0]))
+    for flip, sent in enumerate(sends, 1):
         found.append(lax.ppermute(sent, "band", [(b, b ^ flip) for b in range(bands)]))
     return found
 
@@ -128,12 +133,15 @@
 
 
 def pick(slots_ref, arrays, target):
-    for step in range(target.shape[0]):
-        for slot, array in enumerate(arrays):
+    count, _, _ = target.shape
+    height = arrays[0].shape[0]
+    for step in range(count):
+        for place, array in enumerate(arrays):
+            piece, slot = divmod(place, count)
 
             @pl.when(slots_ref[step] == slot)
             def _():
-                target[step] = array[...]
+                target[step, pl.ds(piece * height, height), :] = array[...]
 
 
 def cross_kernel(*refs):
@@ -180,8 +188,8 @@
 def apply_kernel(scale, per, part_count, *refs):
     tables = refs[:4]
     crosses = refs[4 : 4 + part_count]
-    links = refs[4 + part_count : -5]
-    w_ref, x_ref, out_ref, link_high, link_low = refs[-5:]
+    links = refs[4 + part_count : -4]
+    w_ref, x_ref, out_ref, link_ref = refs[-4:]
     count, rows, cols = crosses[0].shape
 
     @pl.when(pl.program_id(0) == 0)
@@ -189,7 +197,7 @@
         total = links[0][...]
         for part in links[1:]:
             total = total + part[...]
-        link_high[...], link_low[...] = halves(total)
+        link_ref[...] = total.astype(BF16)
 
     applied = []
     field = x_ref[...]
@@ -198,10 +206,8 @@
         total = crosses[0][step]
         for part in crosses[1:]:
             total = total + part[step]
-        for high, low in applied:
-            total = total + (
-                mm(high, link_high[place]) + (mm(high, link_low[place]) + mm(low, link_high[place]))
-            )
+        for high in applied:
+            total = total + mm(high, link_ref[place])
             place += 1
         weight = jnp.concatenate(
             [
@@ -213,8 +219,8 @@
             axis=0,
         )
         change = total * scale * weight
-        applied.append(halves(change))
-        high, low = applied[-1]
+        high, low = halves(change)
+        applied.append(high)
         field = field + (mm(high, w_ref[step]) + mm(low, w_ref[step]))
     out_ref[...] = field
 
@@ -230,7 +236,10 @@
     per = 2 if row_blocks % 2 == 0 else 1
     slots = slots_of(order, arrivals)
     gram_parts = member_parts(nt(obs_anom, obs_anom))
-    ys = gathered(obs_anom, arrivals)
+    half = num_obs // 2
+    held = [innov]
+    ys = gathered(obs_anom[:half], arrivals, early=held)
+    innov = held[0]
     solve = pl.pallas_call(
         functools.partial(weigh_kernel, scale, len(gram_parts)),
         out_shape=jax.ShapeDtypeStruct(innov.shape, BF16),
@@ -243,6 +252,7 @@
     )
     weights = solve(*gram_parts, innov)
     slots, weights = lax.optimization_barrier((slots, weights))
+    ys = ys + gathered(obs_anom[half:], arrivals, tie=weights)
     ws = gathered(weights, arrivals)
     tall = per * rows
     row_spec = pl.BlockSpec((arrivals, tall, num_obs), lambda i: (0, i, 0))
@@ -255,7 +265,7 @@
         out_shape=(cross_shape, jax.ShapeDtypeStruct(batch_shape, BF16)),
         grid=(row_blocks // per,),
         in_specs=[SMEM_SPEC, field_spec]
-        + [pl.BlockSpec(obs_anom.shape, lambda i: (0, 0))] * len(ys),
+        + [pl.BlockSpec(ys[0].shape, lambda i: (0, 0))] * len(ys),
         out_specs=(row_spec, batch_spec),
         cost_estimate=pl.CostEstimate(
             flops=2 * arrivals * state.size * num_obs, bytes_accessed=12 * state.size, transcendentals=0
@@ -287,7 +297,7 @@
         + [pl.BlockSpec(link_shape, lambda i: (0, 0, 0))] * len(links)
         + [batch_spec, field_spec],
         out_specs=field_spec,
-        scratch_shapes=[pltpu.VMEM(link_shape, BF16), pltpu.VMEM(link_shape, BF16)],
+        scratch_shapes=[pltpu.VMEM(link_shape, BF16)],
     )(*tables, *crosses, *links, w_sorted, state)
 
 

time: 120 us -> 122 us (1.017)
  starting transfers between devices: 10.4 us -> 14.9 us
  Pallas kernels: 34 us -> 31.1 us
  waiting for transfers between devices: 66.4 us -> 64.4 us
  local copies, waits for them, and re-layouts: 5.17 us -> 6.57 us
    ppermute x5 -> x6, waiting for transfers between devices: 32.7 us -> 24.1 us  [from_behind(): return lax.ppermute(value, axis, pairs)]
    ppermute x6 -> x9, waiting for transfers between devices: 33.7 us -> 40.3 us  [gathered(): lax.ppermute(sent, 'band', [(b, b ^ flip) for b in range(bands)])]
    ppermute x6 -> x9, starting transfers between devices: 7.11 us -> 10.6 us  [gathered(): lax.ppermute(sent, 'band', [(b, b ^ flip) for b in range(bands)])]
    pallas_call x1, Pallas kernels: 15.6 us -> 12.6 us  [on_device(): pl.pallas_call(functools.partial(apply_kernel, scale, per, len(crosses)),...]
    ppermute x5 -> x6, starting transfers between devices: 3.31 us -> 4.26 us  [from_behind(): return lax.ppermute(value, axis, pairs)]
    unnamed x24 -> x38, local copies, waits for them, and re-layouts: 5.17 us -> 5.53 us
  transfers between devices with their start and end apart: 11 -> 15, of which waited for: 8 -> 8; matrix products, arithmetic and copies ran while one was open for 4% -> 5% of each run, Pallas kernels for 9% -> 9%
where the time goes in v1:
time: 122 us; the launch traced here: 121 us
  waiting for transfers between devices  64.4 us (53%)
  Pallas kernels  31.1 us (25%)
  starting transfers between devices  14.9 us (12%)
  local copies, waits for them, and re-layouts  6.57 us (5%)
  other arithmetic  2.54 us (2%)
  matrix products  1.54 us (1%)
    ppermute x9, waiting for transfers between devices, gathered(): lax.ppermute(sent, 'band', [(b, b ^ flip) for b in range(bands)])  40.3 us
    ppermute x6, waiting for transfers between devices, from_behind(): return lax.ppermute(value, axis, pairs)  24.1 us
    pallas_call x1, Pallas kernels, on_device(): pl.pallas_call(functools.partial(apply_kernel, scale, per, len(crosses)),...  12.6 us
    ppermute x9, starting transfers between devices, gathered(): lax.ppermute(sent, 'band', [(b, b ^ flip) for b in range(bands)])  10.6 us
    pallas_call x1, Pallas kernels, on_device(): cross, y_sorted = cross_call(slots, state, *ys)  7.83 us
    pallas_call x1, Pallas kernels, on_device(): weights = solve(*gram_parts, innov)  6.18 us
    unnamed x38, local copies, waits for them, and re-layouts  5.53 us
    pallas_call x1, Pallas kernels, on_device(): pl.pallas_call(link_kernel, out_shape=(jax.ShapeDtypeStruct(link_shape, F...  4.57 us
  transfers between devices with their start and end apart: 15, of which 8 were waited for; matrix products, arithmetic and copies ran while one was open for 5% of the time, Pallas kernels for 9%

profile of v1, /device:TPU:0, one launch (start us, length us, event | category | flops | bytes accessed | tf_op | source)
XLA Modules:
  0.0 121.2 jit_solution(7806901935835406198)
XLA Ops:
  0.0 1.0 slice.6.refs_2_
  1.0 0.0 copy-start.7
  1.1 3.1 %collective-permute-start.1 = (bf16[128,1024]{1,0:T(8,128)(2,1)S(1)}, bf16[128,1024]{1,0:T(8,128)(2,1)S(1)}, u32[]{:S(2)}, u32[]{:S(2)}) collective-permute-start(bf16[128,1024]{1,0:T(8,128)(2,1)S(1)} %slice.6.refs_2_), channel_id=1, source_target_pairs={{0,8},{2,10},{4,12},{6,14},{8,16},{10,18},{12,20},{14,22},{16,24},... | collective-permute-start | bytes 786440 | tf_op jit(solution)/shard_map/ppermute | solution.py:20
  4.2 1.5 %fusion.2.refs_0_ = f32[256,256]{1,0:T(8,128)S(1)} fusion(bf16[256,1024]{1,0:T(8,128)(2,1)} %param.8), kind=kOutput, calls=%fused_computation.14 | convolution fusion | flops 134217728 | bytes 786432 | tf_op jit(solution)/shard_map/dot_general | solution.py:49
  5.7 0.0 copy-start.6
  5.7 0.1 collective-permute-start
  5.8 6.7 %collective-permute-done.1 = bf16[128,1024]{1,0:T(8,128)(2,1)S(1)} collective-permute-done((bf16[128,1024]{1,0:T(8,128)(2,1)S(1)}, bf16[128,1024]{1,0:T(8,128)(2,1)S(1)}, u32[]{:S(2)}, u32[]{:S(2)}) %collective-permute-start.1) | collective-permute-done | bytes 262176 | tf_op jit(solution)/shard_map/ppermute | solution.py:20
  12.5 1.1 broadcast_select_fusion.4
  13.6 0.0 copy-start.8
  13.6 0.1 collective-permute-start.9
  13.7 1.3 %fusion.refs_0_ = s32[4]{0:T(128)} fusion(s32[1,4]{1,0:T(1,128)} %refs_0_.1, s32[]{:T(128)S(6)} %select_n.71), kind=kLoop, calls=%fused_computation.12 | loop fusion | flops 56 | bytes 36 | tf_op jit(solution)/shard_map/xor | solution.py:132
  15.0 1.5 %collective-permute-start.6 = (bf16[128,1024]{1,0:T(8,128)(2,1)S(1)}, bf16[128,1024]{1,0:T(8,128)(2,1)S(1)}, u32[]{:S(2)}, u32[]{:S(2)}) collective-permute-start(bf16[128,1024]{1,0:T(8,128)(2,1)S(1)} %get-tuple-element.24), channel_id=1, source_target_pairs={{0,2},{2,0},{4,6},{6,4},{8,10},{10,8},{12,14},{14,12},{16,18},{18,... | collective-permute-start | bytes 786440 | tf_op jit(solution)/shard_map/ppermute | solution.py:123
  16.4 0.0 collective-permute-done.refs_1_
  16.4 0.0 copy-done.6
  16.5 0.7 copy-done.11
  17.1 6.2 %shard_map.73.refs_2_ = bf16[256,1024]{1,0:T(8,128)(2,1)} custom-call(f32[256,256]{1,0:T(8,128)} %copy-done.6, f32[256,256]{1,0:T(8,128)} %copy-done.11, f32[256,1024]{1,0:T(8,128)} %refs_2_.1), custom_call_target="tpu_custom_call" | custom-call | flops 1006632960 | bytes 2097152 | tf_op jit(solution)/shard_map/pallas_call | solution.py:253
  23.3 1.5 %collective-permute-start.7 = (bf16[128,1024]{1,0:T(8,128)(2,1)S(1)}, bf16[128,1024]{1,0:T(8,128)(2,1)S(1)}, u32[]{:S(2)}, u32[]{:S(2)}) collective-permute-start(bf16[128,1024]{1,0:T(8,128)(2,1)S(1)} %get-tuple-element.25), channel_id=1, source_target_pairs={{0,4},{2,6},{4,0},{6,2},{8,12},{10,14},{12,8},{14,10},{16,20},{18,... | collective-permute-start | bytes 786440 | tf_op jit(solution)/shard_map/ppermute | solution.py:123
  24.8 0.5 collective-permute-start.8
  25.3 0.0 collective-permute-done.9
  25.3 0.0 copy-done
  25.3 0.1 broadcast_select_fusion.3
  25.4 0.0 copy-start.1
  25.4 2.5 %collective-permute-start.12 = (bf16[128,1024]{1,0:T(8,128)(2,1)S(1)}, bf16[128,1024]{1,0:T(8,128)(2,1)S(1)}, u32[]{:S(2)}, u32[]{:S(2)}) collective-permute-start(bf16[128,1024]{1,0:T(8,128)(2,1)S(1)} %get-tuple-element.40), channel_id=1, source_target_pairs={{0,6},{2,4},{4,2},{6,0},{8,14},{10,12},{12,10},{14,8},{16,22},{18,... | collective-permute-start | bytes 786440 | tf_op jit(solution)/shard_map/ppermute | solution.py:123
  27.9 0.5 collective-permute-start.11
  28.4 0.0 collective-permute-done.6.refs_3_
  28.4 0.5 collective-permute-start.10
  29.0 14.8 %collective-permute-done.7.refs_4_ = bf16[128,1024]{1,0:T(8,128)(2,1)S(1)} collective-permute-done((bf16[128,1024]{1,0:T(8,128)(2,1)S(1)}, bf16[128,1024]{1,0:T(8,128)(2,1)S(1)}, u32[]{:S(2)}, u32[]{:S(2)}) %collective-permute-start.7) | collective-permute-done | bytes 262176 | tf_op jit(solution)/shard_map/ppermute | solution.py:123
  43.7 0.0 collective-permute-done.8.refs_5_
  43.7 0.0 collective-permute-done.12.refs_9_
  43.7 0.0 copy-start.15
  43.7 3.4 %collective-permute-done.11.refs_8_ = bf16[128,1024]{1,0:T(8,128)(2,1)S(1)} collective-permute-done((bf16[128,1024]{1,0:T(8,128)(2,1)S(1)}, bf16[128,1024]{1,0:T(8,128)(2,1)S(1)}, u32[]{:S(2)}, u32[]{:S(2)}) %collective-permute-start.11) | collective-permute-done | bytes 262176 | tf_op jit(solution)/shard_map/ppermute | solution.py:123
  47.2 0.0 collective-permute-done.10.refs_7_
  47.2 0.0 copy-done.7
  47.2 0.0 copy-done.8
  47.2 0.0 copy-done.12
  47.2 0.0 copy-done.13
  47.2 0.0 copy-done.14
  47.2 0.0 copy-done.15
  47.2 0.6 copy-done.16
  47.9 0.7 copy-done.17
  48.5 7.8 %shard_map.74 = (f32[4,1024,256]{2,1,0:T(8,128)}, bf16[4,256,1024]{2,1,0:T(8,128)(2,1)}) custom-call(s32[4]{0:T(128)} %fusion.refs_0_, f32[1024,1024]{1,0:T(8,128)} %refs_9_.1, bf16[128,1024]{1,0:T(8,128)(2,1)} %copy-done.7, bf16[128,1024]{1,0:T(8,128)(2,1)} %copy-done.12, bf16[128,1024]{1,0:T(8,128)(2,1)} %copy-done.13, bf16[128,1024]{1,0:T(8,128)(2,1)} %copy-done.14, ...), custom_call_target="tpu_custom_call" | custom-call | flops 2147483648 | bytes 12582912 | tf_op jit(solution)/shard_map/pallas_call | solution.py:274
  56.4 0.0 copy-start.10
  56.4 0.1 collective-permute-start.13
  56.5 0.0 copy-done.1
  56.5 0.9 collective-permute-start.2
  57.4 15.2 %collective-permute-done.2 = bf16[256,1024]{1,0:T(8,128)(2,1)S(1)} collective-permute-done((bf16[256,1024]{1,0:T(8,128)(2,1)S(1)}, bf16[256,1024]{1,0:T(8,128)(2,1)S(1)}, u32[]{:S(2)}, u32[]{:S(2)}) %collective-permute-start.2) | collective-permute-done | bytes 524320 | tf_op jit(solution)/shard_map/ppermute | solution.py:20
  72.6 0.1 broadcast_select_fusion
  72.7 1.5 %collective-permute-start.5 = (bf16[256,1024]{1,0:T(8,128)(2,1)S(1)}, bf16[256,1024]{1,0:T(8,128)(2,1)S(1)}, u32[]{:S(2)}, u32[]{:S(2)}) collective-permute-start(bf16[256,1024]{1,0:T(8,128)(2,1)S(1)} %get-tuple-element.37), channel_id=1, source_target_pairs={{0,6},{2,4},{4,2},{6,0},{8,14},{10,12},{12,10},{14,8},{16,22},{18,... | collective-permute-start | bytes 1572872 | tf_op jit(solution)/shard_map/ppermute | solution.py:123
  74.2 0.7 collective-permute-start.4
  75.0 1.3 %collective-permute-start.3 = (bf16[256,1024]{1,0:T(8,128)(2,1)S(1)}, bf16[256,1024]{1,0:T(8,128)(2,1)S(1)}, u32[]{:S(2)}, u32[]{:S(2)}) collective-permute-start(bf16[256,1024]{1,0:T(8,128)(2,1)S(1)} %get-tuple-element.39), channel_id=1, source_target_pairs={{0,2},{2,0},{4,6},{6,4},{8,10},{10,8},{12,14},{14,12},{16,18},{18,... | collective-permute-start | bytes 1572872 | tf_op jit(solution)/shard_map/ppermute | solution.py:123
  76.3 12.2 %collective-permute-done.5.refs_5_ = bf16[256,1024]{1,0:T(8,128)(2,1)S(1)} collective-permute-done((bf16[256,1024]{1,0:T(8,128)(2,1)S(1)}, bf16[256,1024]{1,0:T(8,128)(2,1)S(1)}, u32[]{:S(2)}, u32[]{:S(2)}) %collective-permute-start.5) | collective-permute-done | bytes 524320 | tf_op jit(solution)/shard_map/ppermute | solution.py:123
  88.5 9.8 %collective-permute-done.4.refs_4_ = bf16[256,1024]{1,0:T(8,128)(2,1)S(1)} collective-permute-done((bf16[256,1024]{1,0:T(8,128)(2,1)S(1)}, bf16[256,1024]{1,0:T(8,128)(2,1)S(1)}, u32[]{:S(2)}, u32[]{:S(2)}) %collective-permute-start.4) | collective-permute-done | bytes 524320 | tf_op jit(solution)/shard_map/ppermute | solution.py:123
  98.3 0.1 collective-permute-done.3.refs_3_
  98.4 0.7 copy-done.4
  99.1 0.2 copy-done.5
  99.3 4.6 %shard_map.75 = (f32[6,256,256]{2,1,0:T(8,128)}, bf16[4,256,1024]{2,1,0:T(8,128)(2,1)}) custom-call(s32[4]{0:T(128)} %fusion.refs_0_, bf16[4,256,1024]{2,1,0:T(8,128)(2,1)} %get-tuple-element.30.refs_1_, bf16[256,1024]{1,0:T(8,128)(2,1)} %shard_map.73.refs_2_, bf16[256,1024]{1,0:T(8,128)(2,1)} %copy-done.5, bf16[256,1024]{1,0:T(8,128)(2,1)} %copy-done.4, ...), custom_call_target="tpu_custom_call" | custom-call | tf_op jit(solution)/shard_map/pallas_call | solution.py:281
  103.9 0.0 collective-permute-start.14
  103.9 0.0 copy-done.9
  103.9 0.7 copy.8.refs_1_
  104.6 0.7 copy.9.refs_2_
  105.3 2.2 %collective-permute-done.14.refs_7_ = f32[6,256,256]{2,1,0:T(8,128)S(1)} collective-permute-done((f32[6,256,256]{2,1,0:T(8,128)}, f32[6,256,256]{2,1,0:T(8,128)S(1)}, u32[]{:S(2)}, u32[]{:S(2)}) %collective-permute-start.14) | collective-permute-done | bytes 1572896 | tf_op jit(solution)/shard_map/ppermute | solution.py:20
  107.5 0.0 collective-permute-done.13.refs_5_
  107.5 1.2 copy-done.2
  108.7 12.6 %shard_map.76 = f32[1024,1024]{1,0:T(8,128)} custom-call(s32[1,4]{1,0:T(1,128)} %refs_0_.1, s32[1,4,8,4]{3,2,1,0:T(8,128)} %copy.8.refs_1_, s32[1,4,8,4]{3,2,1,0:T(8,128)} %copy.9.refs_2_, f32[8]{0:T(128)} %refs_3_.1, f32[4,1024,256]{2,1,0:T(8,128)} %get-tuple-element.29.refs_4_, f32[4,1024,256]{2,1,0:T(8,128)} %collective-permute-done.13.refs_5_, ...), custom_call_target="tpu_custom_call" | custom-call | tf_op jit(solution)/shard_map/pallas_call | solution.py:291
  (14 shorter events, 0.0 us)
Async XLA Ops:
  0.0 25.3 %copy-start = (bf16[256,1024]{1,0:T(8,128)(2,1)S(1)}, bf16[256,1024]{1,0:T(8,128)(2,1)}, u32[]{:S(2)}) copy-start(bf16[256,1024]{1,0:T(8,128)(2,1)} %param.8) | copy-start | bytes 1572868
  1.0 46.1 %copy-start.7 = (bf16[128,1024]{1,0:T(8,128)(2,1)}, bf16[128,1024]{1,0:T(8,128)(2,1)S(1)}, u32[]{:S(2)}) copy-start(bf16[128,1024]{1,0:T(8,128)(2,1)S(1)} %slice.6.refs_2_) | copy-start | bytes 786436
  1.1 11.4 %collective-permute-start.1 = (bf16[128,1024]{1,0:T(8,128)(2,1)S(1)}, bf16[128,1024]{1,0:T(8,128)(2,1)S(1)}, u32[]{:S(2)}, u32[]{:S(2)}) collective-permute-start(bf16[128,1024]{1,0:T(8,128)(2,1)S(1)} %slice.6.refs_2_), channel_id=1, source_target_pairs={{0,8},{2,10},{4,12},{6,14},{8,16},{10,18},{12,20},{14,22},{16,24},... | collective-permute-start | bytes 786440 | tf_op jit(solution)/shard_map/ppermute | solution.py:20
  5.7 10.7 %copy-start.6 = (f32[256,256]{1,0:T(8,128)}, f32[256,256]{1,0:T(8,128)S(1)}, u32[]{:S(2)}) copy-start(f32[256,256]{1,0:T(8,128)S(1)} %fusion.2.refs_0_) | copy-start | bytes 786436
  5.7 10.7 %collective-permute-start = (f32[256,256]{1,0:T(8,128)S(1)}, f32[256,256]{1,0:T(8,128)S(1)}, u32[]{:S(2)}, u32[]{:S(2)}) collective-permute-start(f32[256,256]{1,0:T(8,128)S(1)} %fusion.2.refs_0_), channel_id=1, source_target_pairs={{0,1},{1,0},{2,3},{3,2},{4,5},{5,4},{6,7},{7,6},{8,9},{9,8},{10,11... | collective-permute-start | bytes 786440 | tf_op jit(solution)/shard_map/ppermute | solution.py:20
  13.6 33.6 %copy-start.8 = (bf16[128,1024]{1,0:T(8,128)(2,1)}, bf16[128,1024]{1,0:T(8,128)(2,1)S(1)}, u32[]{:S(2)}) copy-start(bf16[128,1024]{1,0:T(8,128)(2,1)S(1)} %get-tuple-element.46.refs_6_) | copy-start | bytes 786436
  13.6 11.7 %collective-permute-start.9 = (bf16[128,1024]{1,0:T(8,128)(2,1)S(1)}, bf16[128,1024]{1,0:T(8,128)(2,1)S(1)}, u32[]{:S(2)}, u32[]{:S(2)}) collective-permute-start(bf16[128,1024]{1,0:T(8,128)(2,1)S(1)} %get-tuple-element.46.refs_6_), channel_id=1, source_target_pairs={{0,8},{2,10},{4,12},{6,14},{8,16},{10,18},{12,20},{14,22},{16,24},... | collective-permute-start | bytes 786440 | tf_op jit(solution)/shard_map/ppermute | solution.py:20
  15.0 13.5 %collective-permute-start.6 = (bf16[128,1024]{1,0:T(8,128)(2,1)S(1)}, bf16[128,1024]{1,0:T(8,128)(2,1)S(1)}, u32[]{:S(2)}, u32[]{:S(2)}) collective-permute-start(bf16[128,1024]{1,0:T(8,128)(2,1)S(1)} %get-tuple-element.24), channel_id=1, source_target_pairs={{0,2},{2,0},{4,6},{6,4},{8,10},{10,8},{12,14},{14,12},{16,18},{18,... | collective-permute-start | bytes 786440 | tf_op jit(solution)/shard_map/ppermute | solution.py:123
  16.5 0.7 copy-start.11
  23.3 20.4 %collective-permute-start.7 = (bf16[128,1024]{1,0:T(8,128)(2,1)S(1)}, bf16[128,1024]{1,0:T(8,128)(2,1)S(1)}, u32[]{:S(2)}, u32[]{:S(2)}) collective-permute-start(bf16[128,1024]{1,0:T(8,128)(2,1)S(1)} %get-tuple-element.25), channel_id=1, source_target_pairs={{0,4},{2,6},{4,0},{6,2},{8,12},{10,14},{12,8},{14,10},{16,20},{18,... | collective-permute-start | bytes 786440 | tf_op jit(solution)/shard_map/ppermute | solution.py:123
  24.8 18.9 %collective-permute-start.8 = (bf16[128,1024]{1,0:T(8,128)(2,1)S(1)}, bf16[128,1024]{1,0:T(8,128)(2,1)S(1)}, u32[]{:S(2)}, u32[]{:S(2)}) collective-permute-start(bf16[128,1024]{1,0:T(8,128)(2,1)S(1)} %get-tuple-element.26), channel_id=1, source_target_pairs={{0,6},{2,4},{4,2},{6,0},{8,14},{10,12},{12,10},{14,8},{16,22},{18,... | collective-permute-start | bytes 786440 | tf_op jit(solution)/shard_map/ppermute | solution.py:123
  25.4 31.1 %copy-start.1 = (bf16[256,1024]{1,0:T(8,128)(2,1)S(1)}, bf16[256,1024]{1,0:T(8,128)(2,1)}, u32[]{:S(2)}) copy-start(bf16[256,1024]{1,0:T(8,128)(2,1)} %shard_map.73.refs_2_) | copy-start | bytes 1572868
  25.4 18.3 %collective-permute-start.12 = (bf16[128,1024]{1,0:T(8,128)(2,1)S(1)}, bf16[128,1024]{1,0:T(8,128)(2,1)S(1)}, u32[]{:S(2)}, u32[]{:S(2)}) collective-permute-start(bf16[128,1024]{1,0:T(8,128)(2,1)S(1)} %get-tuple-element.40), channel_id=1, source_target_pairs={{0,6},{2,4},{4,2},{6,0},{8,14},{10,12},{12,10},{14,8},{16,22},{18,... | collective-permute-start | bytes 786440 | tf_op jit(solution)/shard_map/ppermute | solution.py:123
  27.9 19.2 %collective-permute-start.11 = (bf16[128,1024]{1,0:T(8,128)(2,1)S(1)}, bf16[128,1024]{1,0:T(8,128)(2,1)S(1)}, u32[]{:S(2)}, u32[]{:S(2)}) collective-permute-start(bf16[128,1024]{1,0:T(8,128)(2,1)S(1)} %get-tuple-element.41), channel_id=1, source_target_pairs={{0,4},{2,6},{4,0},{6,2},{8,12},{10,14},{12,8},{14,10},{16,20},{18,... | collective-permute-start | bytes 786440 | tf_op jit(solution)/shard_map/ppermute | solution.py:123
  28.4 18.8 %copy-start.12 = (bf16[128,1024]{1,0:T(8,128)(2,1)}, bf16[128,1024]{1,0:T(8,128)(2,1)S(1)}, u32[]{:S(2)}) copy-start(bf16[128,1024]{1,0:T(8,128)(2,1)S(1)} %collective-permute-done.6.refs_3_) | copy-start | bytes 786436
  28.4 18.7 %collective-permute-start.10 = (bf16[128,1024]{1,0:T(8,128)(2,1)S(1)}, bf16[128,1024]{1,0:T(8,128)(2,1)S(1)}, u32[]{:S(2)}, u32[]{:S(2)}) collective-permute-start(bf16[128,1024]{1,0:T(8,128)(2,1)S(1)} %get-tuple-element.42), channel_id=1, source_target_pairs={{0,2},{2,0},{4,6},{6,4},{8,10},{10,8},{12,14},{14,12},{16,18},{18,... | collective-permute-start | bytes 786440 | tf_op jit(solution)/shard_map/ppermute | solution.py:123
  43.7 3.5 %copy-start.13 = (bf16[128,1024]{1,0:T(8,128)(2,1)}, bf16[128,1024]{1,0:T(8,128)(2,1)S(1)}, u32[]{:S(2)}) copy-start(bf16[128,1024]{1,0:T(8,128)(2,1)S(1)} %collective-permute-done.7.refs_4_) | copy-start | bytes 786436
  43.7 3.5 %copy-start.14 = (bf16[128,1024]{1,0:T(8,128)(2,1)}, bf16[128,1024]{1,0:T(8,128)(2,1)S(1)}, u32[]{:S(2)}) copy-start(bf16[128,1024]{1,0:T(8,128)(2,1)S(1)} %collective-permute-done.8.refs_5_) | copy-start | bytes 786436
  43.7 3.5 %copy-start.15 = (bf16[128,1024]{1,0:T(8,128)(2,1)}, bf16[128,1024]{1,0:T(8,128)(2,1)S(1)}, u32[]{:S(2)}) copy-start(bf16[128,1024]{1,0:T(8,128)(2,1)S(1)} %collective-permute-done.12.refs_9_) | copy-start | bytes 786436
  47.2 0.7 copy-start.16
  47.8 0.7 copy-start.17
  56.4 47.5 %copy-start.9 = (s32[1,4,8,4]{2,3,1,0:T(4,128)S(1)}, s32[1,4,8,4]{2,3,1,0:T(4,128)}, u32[]{:S(2)}) copy-start(s32[1,4,8,4]{2,3,1,0:T(4,128)} %param.10) | copy-start | bytes 1540
  56.4 48.2 %copy-start.10 = (s32[1,4,8,4]{2,3,1,0:T(4,128)S(1)}, s32[1,4,8,4]{2,3,1,0:T(4,128)}, u32[]{:S(2)}) copy-start(s32[1,4,8,4]{2,3,1,0:T(4,128)} %param.11) | copy-start | bytes 1540
  56.4 51.1 %collective-permute-start.13 = (f32[4,1024,256]{2,1,0:T(8,128)}, f32[4,1024,256]{2,1,0:T(8,128)}, u32[]{:S(2)}, u32[]{:S(2)}) collective-permute-start(f32[4,1024,256]{2,1,0:T(8,128)} %get-tuple-element.29.refs_4_), channel_id=1, source_target_pairs={{0,1},{1,0},{2,3},{3,2},{4,5},{5,4},{6,7},{7,6},{8,9},{9,8},{10,11... | collective-permute-start | bytes 12582920 | tf_op jit(solution)/shard_map/ppermute | solution.py:20
  56.5 16.1 %collective-permute-start.2 = (bf16[256,1024]{1,0:T(8,128)(2,1)S(1)}, bf16[256,1024]{1,0:T(8,128)(2,1)S(1)}, u32[]{:S(2)}, u32[]{:S(2)}) collective-permute-start(bf16[256,1024]{1,0:T(8,128)(2,1)S(1)} %copy-done.1), channel_id=1, source_target_pairs={{0,8},{2,10},{4,12},{6,14},{8,16},{10,18},{12,20},{14,22},{16,24},... | collective-permute-start | bytes 1572872 | tf_op jit(solution)/shard_map/ppermute | solution.py:20
  72.7 15.8 %collective-permute-start.5 = (bf16[256,1024]{1,0:T(8,128)(2,1)S(1)}, bf16[256,1024]{1,0:T(8,128)(2,1)S(1)}, u32[]{:S(2)}, u32[]{:S(2)}) collective-permute-start(bf16[256,1024]{1,0:T(8,128)(2,1)S(1)} %get-tuple-element.37), channel_id=1, source_target_pairs={{0,6},{2,4},{4,2},{6,0},{8,14},{10,12},{12,10},{14,8},{16,22},{18,... | collective-permute-start | bytes 1572872 | tf_op jit(solution)/shard_map/ppermute | solution.py:123
  74.2 24.1 %collective-permute-start.4 = (bf16[256,1024]{1,0:T(8,128)(2,1)S(1)}, bf16[256,1024]{1,0:T(8,128)(2,1)S(1)}, u32[]{:S(2)}, u32[]{:S(2)}) collective-permute-start(bf16[256,1024]{1,0:T(8,128)(2,1)S(1)} %get-tuple-element.38), channel_id=1, source_target_pairs={{0,4},{2,6},{4,0},{6,2},{8,12},{10,14},{12,8},{14,10},{16,20},{18,... | collective-permute-start | bytes 1572872 | tf_op jit(solution)/shard_map/ppermute | solution.py:123
  75.0 23.4 %collective-permute-start.3 = (bf16[256,1024]{1,0:T(8,128)(2,1)S(1)}, bf16[256,1024]{1,0:T(8,128)(2,1)S(1)}, u32[]{:S(2)}, u32[]{:S(2)}) collective-permute-start(bf16[256,1024]{1,0:T(8,128)(2,1)S(1)} %get-tuple-element.39), channel_id=1, source_target_pairs={{0,2},{2,0},{4,6},{6,4},{8,10},{10,8},{12,14},{14,12},{16,18},{18,... | collective-permute-start | bytes 1572872 | tf_op jit(solution)/shard_map/ppermute | solution.py:123
  88.5 9.9 %copy-start.3 = (bf16[256,1024]{1,0:T(8,128)(2,1)}, bf16[256,1024]{1,0:T(8,128)(2,1)S(1)}, u32[]{:S(2)}) copy-start(bf16[256,1024]{1,0:T(8,128)(2,1)S(1)} %collective-permute-done.5.refs_5_) | copy-start | bytes 1572868
  98.3 0.8 copy-start.4
  98.4 0.9 copy-start.5
  103.9 3.6 %collective-permute-start.14 = (f32[6,256,256]{2,1,0:T(8,128)}, f32[6,256,256]{2,1,0:T(8,128)S(1)}, u32[]{:S(2)}, u32[]{:S(2)}) collective-permute-start(f32[6,256,256]{2,1,0:T(8,128)} %get-tuple-element.35.refs_6_), channel_id=1, source_target_pairs={{0,1},{1,0},{2,3},{3,2},{4,5},{5,4},{6,7},{7,6},{8,9},{9,8},{10,11... | collective-permute-start | bytes 4718600 | tf_op jit(solution)/shard_map/ppermute | solution.py:20
  107.5 1.2 copy-start.2

commit v2 on v1

--- a/solution.py
+++ b/solution.py
@@ -105,20 +105,16 @@
     return bands % group == 0 and bands > group and group & (group - 1) == 0
 
 
-def gathered(value, group, tie=None, early=None):
+def gathered(value, group):
     bands = lax.axis_size("band")
     if not grouped(group, bands):
         return [value] + [from_behind(value, "band", a) for a in range(1, group)]
     prior = from_behind(value, "band", group)
-    if tie is not None:
-        _, prior = lax.optimization_barrier((tie, prior))
     place = lax.axis_index("band") % group
     found = [value]
     sends = [
         jnp.where((place ^ flip) > place, value, prior) for flip in range(1, group)
     ]
-    if early is not None:
-        sends, early[0] = lax.optimization_barrier((sends, early[0]))
     for flip, sent in enumerate(sends, 1):
         found.append(lax.ppermute(sent, "band", [(b, b ^ flip) for b in range(bands)]))
     return found
@@ -236,10 +232,7 @@
     per = 2 if row_blocks % 2 == 0 else 1
     slots = slots_of(order, arrivals)
     gram_parts = member_parts(nt(obs_anom, obs_anom))
-    half = num_obs // 2
-    held = [innov]
-    ys = gathered(obs_anom[:half], arrivals, early=held)
-    innov = held[0]
+    ys = gathered(obs_anom, arrivals)
     solve = pl.pallas_call(
         functools.partial(weigh_kernel, scale, len(gram_parts)),
         out_shape=jax.ShapeDtypeStruct(innov.shape, BF16),
@@ -252,7 +245,6 @@
     )
     weights = solve(*gram_parts, innov)
     slots, weights = lax.optimization_barrier((slots, weights))
-    ys = ys + gathered(obs_anom[half:], arrivals, tie=weights)
     ws = gathered(weights, arrivals)
     tall = per * rows
     row_spec = pl.BlockSpec((arrivals, tall, num_obs), lambda i: (0, i, 0))

time: 122 us -> 117 us (0.959)
  starting transfers between devices: 14.9 us -> 10.4 us
  waiting for transfers between devices: 64.4 us -> 66.4 us
  local copies, waits for them, and re-layouts: 6.57 us -> 5.17 us
    ppermute x6 -> x5, waiting for transfers between devices: 24.1 us -> 32.7 us  [from_behind(): return lax.ppermute(value, axis, pairs)]
    ppermute x9 -> x6, waiting for transfers between devices: 40.3 us -> 33.7 us  [gathered(): lax.ppermute(sent, 'band', [(b, b ^ flip) for b in range(bands)])]
    ppermute x9 -> x6, starting transfers between devices: 10.6 us -> 7.11 us  [gathered(): lax.ppermute(sent, 'band', [(b, b ^ flip) for b in range(bands)])]
    ppermute x6 -> x5, starting transfers between devices: 4.26 us -> 3.31 us  [from_behind(): return lax.ppermute(value, axis, pairs)]
    unnamed x38 -> x24, local copies, waits for them, and re-layouts: 5.53 us -> 5.17 us
  transfers between devices with their start and end apart: 15 -> 11, of which waited for: 8 -> 8; matrix products, arithmetic and copies ran while one was open for 5% -> 4% of each run, Pallas kernels for 9% -> 9%
where the time goes in v2:
time: 117 us
  waiting for transfers between devices  66.4 us (57%)
  Pallas kernels  31 us (26%)
  starting transfers between devices  10.4 us (9%)
  local copies, waits for them, and re-layouts  5.17 us (4%)
  other arithmetic  2.48 us (2%)
  matrix products  1.54 us (1%)
    ppermute x6, waiting for transfers between devices, gathered(): lax.ppermute(sent, 'band', [(b, b ^ flip) for b in range(bands)])  33.7 us
    ppermute x5, waiting for transfers between devices, from_behind(): return lax.ppermute(value, axis, pairs)  32.7 us
    pallas_call x1, Pallas kernels, on_device(): pl.pallas_call(functools.partial(apply_kernel, scale, per, len(crosses)),...  12.6 us
    pallas_call x1, Pallas kernels, on_device(): cross, y_sorted = cross_call(slots, state, *ys)  7.72 us
    ppermute x6, starting transfers between devices, gathered(): lax.ppermute(sent, 'band', [(b, b ^ flip) for b in range(bands)])  7.11 us
    pallas_call x1, Pallas kernels, on_device(): weights = solve(*gram_parts, innov)  6.18 us
    unnamed x24, local copies, waits for them, and re-layouts  5.17 us
    pallas_call x1, Pallas kernels, on_device(): pl.pallas_call(link_kernel, out_shape=(jax.ShapeDtypeStruct(link_shape, F...  4.54 us
  transfers between devices with their start and end apart: 11, of which 8 were waited for; matrix products, arithmetic and copies ran while one was open for 4% of the time, Pallas kernels for 9%

profile of v2, /device:TPU:0, one launch (start us, length us, event | category | flops | bytes accessed | tf_op | source)
XLA Modules:
  0.0 117.1 jit_solution(14312725978982246358)
XLA Ops:
  0.0 3.1 %collective-permute-start.5 = (bf16[256,1024]{1,0:T(8,128)(2,1)}, bf16[256,1024]{1,0:T(8,128)(2,1)S(1)}, u32[]{:S(2)}, u32[]{:S(2)}) collective-permute-start(bf16[256,1024]{1,0:T(8,128)(2,1)} %refs_2_.4), channel_id=1, source_target_pairs={{0,8},{2,10},{4,12},{6,14},{8,16},{10,18},{12,20},{14,22},{16,24},... | collective-permute-start | bytes 1572872 | tf_op jit(solution)/shard_map/ppermute | solution.py:20
  3.1 14.2 %collective-permute-done.5 = bf16[256,1024]{1,0:T(8,128)(2,1)S(1)} collective-permute-done((bf16[256,1024]{1,0:T(8,128)(2,1)}, bf16[256,1024]{1,0:T(8,128)(2,1)S(1)}, u32[]{:S(2)}, u32[]{:S(2)}) %collective-permute-start.5) | collective-permute-done | bytes 524320 | tf_op jit(solution)/shard_map/ppermute | solution.py:20
  17.2 1.1 broadcast_select_fusion
  18.4 2.5 %collective-permute-start.8 = (bf16[256,1024]{1,0:T(8,128)(2,1)S(1)}, bf16[256,1024]{1,0:T(8,128)(2,1)S(1)}, u32[]{:S(2)}, u32[]{:S(2)}) collective-permute-start(bf16[256,1024]{1,0:T(8,128)(2,1)S(1)} %get-tuple-element.27), channel_id=1, source_target_pairs={{0,6},{2,4},{4,2},{6,0},{8,14},{10,12},{12,10},{14,8},{16,22},{18,... | collective-permute-start | bytes 1572872 | tf_op jit(solution)/shard_map/ppermute | solution.py:119
  20.9 0.5 collective-permute-start.7
  21.4 0.5 collective-permute-start.6
  21.9 1.5 %fusion.2.refs_0_ = f32[256,256]{1,0:T(8,128)S(1)} fusion(bf16[256,1024]{1,0:T(8,128)(2,1)} %refs_2_.4), kind=kOutput, calls=%fused_computation.11 | convolution fusion | flops 134217728 | bytes 786432 | tf_op jit(solution)/shard_map/dot_general | solution.py:49
  23.5 0.0 copy-start.5
  23.5 0.1 collective-permute-start
  23.5 1.2 %fusion.refs_0_ = s32[4]{0:T(128)} fusion(s32[1,4]{1,0:T(1,128)} %refs_0_.1, s32[]{:T(128)S(6)} %select_n.49), kind=kLoop, calls=%fused_computation.9 | loop fusion | flops 56 | bytes 36 | tf_op jit(solution)/shard_map/xor | solution.py:128
  24.8 0.3 collective-permute-done.refs_1_
  25.1 0.0 copy-done.5
  25.1 0.0 copy-start.10
  25.1 0.7 copy-done.10
  25.8 6.2 %shard_map.73.refs_2_ = bf16[256,1024]{1,0:T(8,128)(2,1)} custom-call(f32[256,256]{1,0:T(8,128)} %copy-done.5, f32[256,256]{1,0:T(8,128)} %copy-done.10, f32[256,1024]{1,0:T(8,128)} %refs_2_.3), custom_call_target="tpu_custom_call" | custom-call | flops 1006632960 | bytes 2097152 | tf_op jit(solution)/shard_map/pallas_call | solution.py:246
  32.0 0.0 copy-start
  32.0 2.2 %collective-permute-done.8.refs_5_ = bf16[256,1024]{1,0:T(8,128)(2,1)S(1)} collective-permute-done((bf16[256,1024]{1,0:T(8,128)(2,1)S(1)}, bf16[256,1024]{1,0:T(8,128)(2,1)S(1)}, u32[]{:S(2)}, u32[]{:S(2)}) %collective-permute-start.8) | collective-permute-done | bytes 524320 | tf_op jit(solution)/shard_map/ppermute | solution.py:119
  34.2 0.0 copy-start.8
  34.2 9.5 %collective-permute-done.7.refs_4_ = bf16[256,1024]{1,0:T(8,128)(2,1)S(1)} collective-permute-done((bf16[256,1024]{1,0:T(8,128)(2,1)S(1)}, bf16[256,1024]{1,0:T(8,128)(2,1)S(1)}, u32[]{:S(2)}, u32[]{:S(2)}) %collective-permute-start.7) | collective-permute-done | bytes 524320 | tf_op jit(solution)/shard_map/ppermute | solution.py:119
  43.6 0.0 copy-start.9
  43.6 0.0 collective-permute-done.6.refs_3_
  43.7 0.0 copy-done.8
  43.7 0.8 copy-done.9
  44.4 7.7 %shard_map.74 = (f32[4,1024,256]{2,1,0:T(8,128)}, bf16[4,256,1024]{2,1,0:T(8,128)(2,1)}) custom-call(s32[4]{0:T(128)} %fusion.refs_0_, f32[1024,1024]{1,0:T(8,128)} %refs_9_.1, bf16[256,1024]{1,0:T(8,128)(2,1)} %refs_2_.4, bf16[256,1024]{1,0:T(8,128)(2,1)} %collective-permute-done.6.refs_3_, bf16[256,1024]{1,0:T(8,128)(2,1)} %copy-done.9, ...), custom_call_target="tpu_custom_call" | custom-call | flops 2147483648 | bytes 12582912 | tf_op jit(solution)/shard_map/pallas_call | solution.py:266
  52.2 0.0 copy-start.6
  52.2 0.0 copy-start.7
  52.2 0.2 collective-permute-start.9
  52.4 0.0 copy-done
  52.4 0.0 collective-permute-start.1
  52.4 16.0 %collective-permute-done.1 = bf16[256,1024]{1,0:T(8,128)(2,1)S(1)} collective-permute-done((bf16[256,1024]{1,0:T(8,128)(2,1)S(1)}, bf16[256,1024]{1,0:T(8,128)(2,1)S(1)}, u32[]{:S(2)}, u32[]{:S(2)}) %collective-permute-start.1) | collective-permute-done | bytes 524320 | tf_op jit(solution)/shard_map/ppermute | solution.py:20
  68.4 0.1 broadcast_select_fusion.1
  68.5 1.8 %collective-permute-start.4 = (bf16[256,1024]{1,0:T(8,128)(2,1)S(1)}, bf16[256,1024]{1,0:T(8,128)(2,1)S(1)}, u32[]{:S(2)}, u32[]{:S(2)}) collective-permute-start(bf16[256,1024]{1,0:T(8,128)(2,1)S(1)} %get-tuple-element.30), channel_id=1, source_target_pairs={{0,6},{2,4},{4,2},{6,0},{8,14},{10,12},{12,10},{14,8},{16,22},{18,... | collective-permute-start | bytes 1572872 | tf_op jit(solution)/shard_map/ppermute | solution.py:119
  70.3 1.0 collective-permute-start.3
  71.3 0.8 collective-permute-start.2
  72.1 12.2 %collective-permute-done.4.refs_5_ = bf16[256,1024]{1,0:T(8,128)(2,1)S(1)} collective-permute-done((bf16[256,1024]{1,0:T(8,128)(2,1)S(1)}, bf16[256,1024]{1,0:T(8,128)(2,1)S(1)}, u32[]{:S(2)}, u32[]{:S(2)}) %collective-permute-start.4) | collective-permute-done | bytes 524320 | tf_op jit(solution)/shard_map/ppermute | solution.py:119
  84.3 0.0 copy-start.2
  84.3 9.8 %collective-permute-done.3.refs_4_ = bf16[256,1024]{1,0:T(8,128)(2,1)S(1)} collective-permute-done((bf16[256,1024]{1,0:T(8,128)(2,1)S(1)}, bf16[256,1024]{1,0:T(8,128)(2,1)S(1)}, u32[]{:S(2)}, u32[]{:S(2)}) %collective-permute-start.3) | collective-permute-done | bytes 524320 | tf_op jit(solution)/shard_map/ppermute | solution.py:119
  94.1 0.0 copy-start.3
  94.1 0.0 collective-permute-done.2.refs_3_
  94.1 0.0 copy-start.4
  94.1 0.0 copy-done.2
  94.1 0.8 copy-done.3
  94.9 0.2 copy-done.4
  95.1 4.5 %shard_map.75 = (f32[6,256,256]{2,1,0:T(8,128)}, bf16[4,256,1024]{2,1,0:T(8,128)(2,1)}) custom-call(s32[4]{0:T(128)} %fusion.refs_0_, bf16[4,256,1024]{2,1,0:T(8,128)(2,1)} %get-tuple-element.20.refs_1_, bf16[256,1024]{1,0:T(8,128)(2,1)} %shard_map.73.refs_2_, bf16[256,1024]{1,0:T(8,128)(2,1)} %copy-done.4, bf16[256,1024]{1,0:T(8,128)(2,1)} %copy-done.3, ...), custom_call_target="tpu_custom_call" | custom-call | tf_op jit(solution)/shard_map/pallas_call | solution.py:273
  99.7 0.0 collective-permute-start.10
  99.7 0.0 copy-done.6
  99.7 0.7 copy.8.refs_1_
  100.4 0.0 copy-done.7
  100.4 0.7 copy.9.refs_2_
  101.1 2.2 %collective-permute-done.10.refs_7_ = f32[6,256,256]{2,1,0:T(8,128)S(1)} collective-permute-done((f32[6,256,256]{2,1,0:T(8,128)}, f32[6,256,256]{2,1,0:T(8,128)S(1)}, u32[]{:S(2)}, u32[]{:S(2)}) %collective-permute-start.10) | collective-permute-done | bytes 1572896 | tf_op jit(solution)/shard_map/ppermute | solution.py:20
  103.3 0.0 copy-start.1
  103.3 0.0 collective-permute-done.9.refs_5_
  103.3 1.2 %copy-done.1 = f32[6,256,256]{2,1,0:T(8,128)} copy-done((f32[6,256,256]{2,1,0:T(8,128)}, f32[6,256,256]{2,1,0:T(8,128)S(1)}, u32[]{:S(2)}) %copy-start.1) | copy-done | bytes 1572888
  104.5 12.6 %shard_map.76 = f32[1024,1024]{1,0:T(8,128)} custom-call(s32[1,4]{1,0:T(1,128)} %refs_0_.1, s32[1,4,8,4]{3,2,1,0:T(8,128)} %copy.8.refs_1_, s32[1,4,8,4]{3,2,1,0:T(8,128)} %copy.9.refs_2_, f32[8]{0:T(128)} %refs_3_.1, f32[4,1024,256]{2,1,0:T(8,128)} %get-tuple-element.19.refs_4_, f32[4,1024,256]{2,1,0:T(8,128)} %collective-permute-done.9.refs_5_, ...), custom_call_target="tpu_custom_call" | custom-call | tf_op jit(solution)/shard_map/pallas_call | solution.py:283
Async XLA Ops:
  0.0 17.2 %collective-permute-start.5 = (bf16[256,1024]{1,0:T(8,128)(2,1)}, bf16[256,1024]{1,0:T(8,128)(2,1)S(1)}, u32[]{:S(2)}, u32[]{:S(2)}) collective-permute-start(bf16[256,1024]{1,0:T(8,128)(2,1)} %refs_2_.4), channel_id=1, source_target_pairs={{0,8},{2,10},{4,12},{6,14},{8,16},{10,18},{12,20},{14,22},{16,24},... | collective-permute-start | bytes 1572872 | tf_op jit(solution)/shard_map/ppermute | solution.py:20
  18.4 15.8 %collective-permute-start.8 = (bf16[256,1024]{1,0:T(8,128)(2,1)S(1)}, bf16[256,1024]{1,0:T(8,128)(2,1)S(1)}, u32[]{:S(2)}, u32[]{:S(2)}) collective-permute-start(bf16[256,1024]{1,0:T(8,128)(2,1)S(1)} %get-tuple-element.27), channel_id=1, source_target_pairs={{0,6},{2,4},{4,2},{6,0},{8,14},{10,12},{12,10},{14,8},{16,22},{18,... | collective-permute-start | bytes 1572872 | tf_op jit(solution)/shard_map/ppermute | solution.py:119
  20.9 22.8 %collective-permute-start.7 = (bf16[256,1024]{1,0:T(8,128)(2,1)S(1)}, bf16[256,1024]{1,0:T(8,128)(2,1)S(1)}, u32[]{:S(2)}, u32[]{:S(2)}) collective-permute-start(bf16[256,1024]{1,0:T(8,128)(2,1)S(1)} %get-tuple-element.28), channel_id=1, source_target_pairs={{0,4},{2,6},{4,0},{6,2},{8,12},{10,14},{12,8},{14,10},{16,20},{18,... | collective-permute-start | bytes 1572872 | tf_op jit(solution)/shard_map/ppermute | solution.py:119
  21.4 22.3 %collective-permute-start.6 = (bf16[256,1024]{1,0:T(8,128)(2,1)S(1)}, bf16[256,1024]{1,0:T(8,128)(2,1)}, u32[]{:S(2)}, u32[]{:S(2)}) collective-permute-start(bf16[256,1024]{1,0:T(8,128)(2,1)S(1)} %get-tuple-element.29), channel_id=1, source_target_pairs={{0,2},{2,0},{4,6},{6,4},{8,10},{10,8},{12,14},{14,12},{16,18},{18,... | collective-permute-start | bytes 1572872 | tf_op jit(solution)/shard_map/ppermute | solution.py:119
  23.5 1.6 %copy-start.5 = (f32[256,256]{1,0:T(8,128)}, f32[256,256]{1,0:T(8,128)S(1)}, u32[]{:S(2)}) copy-start(f32[256,256]{1,0:T(8,128)S(1)} %fusion.2.refs_0_) | copy-start | bytes 786436
  23.5 1.6 %collective-permute-start = (f32[256,256]{1,0:T(8,128)S(1)}, f32[256,256]{1,0:T(8,128)S(1)}, u32[]{:S(2)}, u32[]{:S(2)}) collective-permute-start(f32[256,256]{1,0:T(8,128)S(1)} %fusion.2.refs_0_), channel_id=1, source_target_pairs={{0,1},{1,0},{2,3},{3,2},{4,5},{5,4},{6,7},{7,6},{8,9},{9,8},{10,11... | collective-permute-start | bytes 786440 | tf_op jit(solution)/shard_map/ppermute | solution.py:20
  25.1 0.7 copy-start.10
  32.0 20.4 %copy-start = (bf16[256,1024]{1,0:T(8,128)(2,1)S(1)}, bf16[256,1024]{1,0:T(8,128)(2,1)}, u32[]{:S(2)}) copy-start(bf16[256,1024]{1,0:T(8,128)(2,1)} %shard_map.73.refs_2_) | copy-start | bytes 1572868
  34.2 9.5 %copy-start.8 = (bf16[256,1024]{1,0:T(8,128)(2,1)}, bf16[256,1024]{1,0:T(8,128)(2,1)S(1)}, u32[]{:S(2)}) copy-start(bf16[256,1024]{1,0:T(8,128)(2,1)S(1)} %collective-permute-done.8.refs_5_) | copy-start | bytes 1572868
  43.6 0.8 copy-start.9
  52.2 47.5 %copy-start.6 = (s32[1,4,8,4]{2,3,1,0:T(4,128)S(1)}, s32[1,4,8,4]{2,3,1,0:T(4,128)}, u32[]{:S(2)}) copy-start(s32[1,4,8,4]{2,3,1,0:T(4,128)} %param.10) | copy-start | bytes 1540
  52.2 48.2 %copy-start.7 = (s32[1,4,8,4]{2,3,1,0:T(4,128)S(1)}, s32[1,4,8,4]{2,3,1,0:T(4,128)}, u32[]{:S(2)}) copy-start(s32[1,4,8,4]{2,3,1,0:T(4,128)} %param.11) | copy-start | bytes 1540
  52.2 51.1 %collective-permute-start.9 = (f32[4,1024,256]{2,1,0:T(8,128)}, f32[4,1024,256]{2,1,0:T(8,128)}, u32[]{:S(2)}, u32[]{:S(2)}) collective-permute-start(f32[4,1024,256]{2,1,0:T(8,128)} %get-tuple-element.19.refs_4_), channel_id=1, source_target_pairs={{0,1},{1,0},{2,3},{3,2},{4,5},{5,4},{6,7},{7,6},{8,9},{9,8},{10,11... | collective-permute-start | bytes 12582920 | tf_op jit(solution)/shard_map/ppermute | solution.py:20
  52.4 16.0 %collective-permute-start.1 = (bf16[256,1024]{1,0:T(8,128)(2,1)S(1)}, bf16[256,1024]{1,0:T(8,128)(2,1)S(1)}, u32[]{:S(2)}, u32[]{:S(2)}) collective-permute-start(bf16[256,1024]{1,0:T(8,128)(2,1)S(1)} %copy-done), channel_id=1, source_target_pairs={{0,8},{2,10},{4,12},{6,14},{8,16},{10,18},{12,20},{14,22},{16,24},... | collective-permute-start | bytes 1572872 | tf_op jit(solution)/shard_map/ppermute | solution.py:20
  68.5 15.8 %collective-permute-start.4 = (bf16[256,1024]{1,0:T(8,128)(2,1)S(1)}, bf16[256,1024]{1,0:T(8,128)(2,1)S(1)}, u32[]{:S(2)}, u32[]{:S(2)}) collective-permute-start(bf16[256,1024]{1,0:T(8,128)(2,1)S(1)} %get-tuple-element.30), channel_id=1, source_target_pairs={{0,6},{2,4},{4,2},{6,0},{8,14},{10,12},{12,10},{14,8},{16,22},{18,... | collective-permute-start | bytes 1572872 | tf_op jit(solution)/shard_map/ppermute | solution.py:119
  70.3 23.8 %collective-permute-start.3 = (bf16[256,1024]{1,0:T(8,128)(2,1)S(1)}, bf16[256,1024]{1,0:T(8,128)(2,1)S(1)}, u32[]{:S(2)}, u32[]{:S(2)}) collective-permute-start(bf16[256,1024]{1,0:T(8,128)(2,1)S(1)} %get-tuple-element.31), channel_id=1, source_target_pairs={{0,4},{2,6},{4,0},{6,2},{8,12},{10,14},{12,8},{14,10},{16,20},{18,... | collective-permute-start | bytes 1572872 | tf_op jit(solution)/shard_map/ppermute | solution.py:119
  71.3 22.8 %collective-permute-start.2 = (bf16[256,1024]{1,0:T(8,128)(2,1)S(1)}, bf16[256,1024]{1,0:T(8,128)(2,1)S(1)}, u32[]{:S(2)}, u32[]{:S(2)}) collective-permute-start(bf16[256,1024]{1,0:T(8,128)(2,1)S(1)} %get-tuple-element.32), channel_id=1, source_target_pairs={{0,2},{2,0},{4,6},{6,4},{8,10},{10,8},{12,14},{14,12},{16,18},{18,... | collective-permute-start | bytes 1572872 | tf_op jit(solution)/shard_map/ppermute | solution.py:119
  84.3 9.8 %copy-start.2 = (bf16[256,1024]{1,0:T(8,128)(2,1)}, bf16[256,1024]{1,0:T(8,128)(2,1)S(1)}, u32[]{:S(2)}) copy-start(bf16[256,1024]{1,0:T(8,128)(2,1)S(1)} %collective-permute-done.4.refs_5_) | copy-start | bytes 1572868
  94.1 0.8 copy-start.3
  94.1 1.0 copy-start.4
  99.7 3.6 %collective-permute-start.10 = (f32[6,256,256]{2,1,0:T(8,128)}, f32[6,256,256]{2,1,0:T(8,128)S(1)}, u32[]{:S(2)}, u32[]{:S(2)}) collective-permute-start(f32[6,256,256]{2,1,0:T(8,128)} %get-tuple-element.25.refs_6_), channel_id=1, source_target_pairs={{0,1},{1,0},{2,3},{3,2},{4,5},{5,4},{6,7},{7,6},{8,9},{9,8},{10,11... | collective-permute-start | bytes 4718600 | tf_op jit(solution)/shard_map/ppermute | solution.py:20
  103.3 1.2 %copy-start.1 = (f32[6,256,256]{2,1,0:T(8,128)}, f32[6,256,256]{2,1,0:T(8,128)S(1)}, u32[]{:S(2)}) copy-start(f32[6,256,256]{2,1,0:T(8,128)S(1)} %collective-permute-done.10.refs_7_) | copy-start | bytes 4718596

commit v3 on v2

--- a/solution.py
+++ b/solution.py
@@ -177,7 +177,7 @@
     place = 0
     for step in range(1, y_ref.shape[0]):
         for before in range(step):
-            g_ref[place] = nt(w_ref[before], y_ref[step])
+            g_ref[place] = nt(w_ref[before], y_ref[step]).astype(BF16)
             place += 1
 
 
@@ -190,9 +190,9 @@
 
     @pl.when(pl.program_id(0) == 0)
     def _():
-        total = links[0][...]
+        total = links[0][...].astype(F32)
         for part in links[1:]:
-            total = total + part[...]
+            total = total + part[...].astype(F32)
         link_ref[...] = total.astype(BF16)
 
     applied = []
@@ -273,7 +273,7 @@
     link, w_sorted = pl.pallas_call(
         link_kernel,
         out_shape=(
-            jax.ShapeDtypeStruct(link_shape, F32),
+            jax.ShapeDtypeStruct(link_shape, BF16),
             jax.ShapeDtypeStruct(batch_shape, BF16),
         ),
         in_specs=[SMEM_SPEC] + [VMEM_SPEC] * (1 + len(ws)),

time: 117 us -> 115 us (0.983)
    ppermute x5, waiting for transfers between devices: 32.7 us -> 31.5 us  [from_behind(): return lax.ppermute(value, axis, pairs)]
where the time goes in v3:
time: 115 us
  waiting for transfers between devices  65.3 us (57%)
  Pallas kernels  30.3 us (26%)
  starting transfers between devices  10.4 us (9%)
  local copies, waits for them, and re-layouts  4.79 us (4%)
  other arithmetic  2.53 us (2%)
  matrix products  1.54 us (1%)
    ppermute x6, waiting for transfers between devices, gathered(): lax.ppermute(sent, 'band', [(b, b ^ flip) for b in range(bands)])  33.7 us
    ppermute x5, waiting for transfers between devices, from_behind(): return lax.ppermute(value, axis, pairs)  31.5 us
    pallas_call x1, Pallas kernels, on_device(): pl.pallas_call(functools.partial(apply_kernel, scale, per, len(crosses)),...  12.1 us
    pallas_call x1, Pallas kernels, on_device(): cross, y_sorted = cross_call(slots, state, *ys)  7.72 us
    ppermute x6, starting transfers between devices, gathered(): lax.ppermute(sent, 'band', [(b, b ^ flip) for b in range(bands)])  7.11 us
    pallas_call x1, Pallas kernels, on_device(): weights = solve(*gram_parts, innov)  6.16 us
    unnamed x24, local copies, waits for them, and re-layouts  4.79 us
    pallas_call x1, Pallas kernels, on_device(): pl.pallas_call(link_kernel, out_shape=(jax.ShapeDtypeStruct(link_shape, B...  4.31 us
  transfers between devices with their start and end apart: 11, of which 8 were waited for; matrix products, arithmetic and copies ran while one was open for 4% of the time, Pallas kernels for 9%

profile of v3, /device:TPU:0, one launch (start us, length us, event | category | flops | bytes accessed | tf_op | source)
XLA Modules:
  0.0 114.9 jit_solution(4266909645269680342)
XLA Ops:
  0.0 3.1 %collective-permute-start.5 = (bf16[256,1024]{1,0:T(8,128)(2,1)}, bf16[256,1024]{1,0:T(8,128)(2,1)S(1)}, u32[]{:S(2)}, u32[]{:S(2)}) collective-permute-start(bf16[256,1024]{1,0:T(8,128)(2,1)} %refs_2_.4), channel_id=1, source_target_pairs={{0,8},{2,10},{4,12},{6,14},{8,16},{10,18},{12,20},{14,22},{16,24},... | collective-permute-start | bytes 1572872 | tf_op jit(solution)/shard_map/ppermute | solution.py:20
  3.1 14.2 %collective-permute-done.5 = bf16[256,1024]{1,0:T(8,128)(2,1)S(1)} collective-permute-done((bf16[256,1024]{1,0:T(8,128)(2,1)}, bf16[256,1024]{1,0:T(8,128)(2,1)S(1)}, u32[]{:S(2)}, u32[]{:S(2)}) %collective-permute-start.5) | collective-permute-done | bytes 524320 | tf_op jit(solution)/shard_map/ppermute | solution.py:20
  17.2 1.1 broadcast_select_fusion
  18.4 2.5 %collective-permute-start.8 = (bf16[256,1024]{1,0:T(8,128)(2,1)S(1)}, bf16[256,1024]{1,0:T(8,128)(2,1)S(1)}, u32[]{:S(2)}, u32[]{:S(2)}) collective-permute-start(bf16[256,1024]{1,0:T(8,128)(2,1)S(1)} %get-tuple-element.27), channel_id=1, source_target_pairs={{0,6},{2,4},{4,2},{6,0},{8,14},{10,12},{12,10},{14,8},{16,22},{18,... | collective-permute-start | bytes 1572872 | tf_op jit(solution)/shard_map/ppermute | solution.py:119
  20.9 0.5 collective-permute-start.7
  21.4 0.5 collective-permute-start.6
  21.9 1.5 %fusion.2.refs_0_ = f32[256,256]{1,0:T(8,128)S(1)} fusion(bf16[256,1024]{1,0:T(8,128)(2,1)} %refs_2_.4), kind=kOutput, calls=%fused_computation.11 | convolution fusion | flops 134217728 | bytes 786432 | tf_op jit(solution)/shard_map/dot_general | solution.py:49
  23.5 0.0 copy-start.5
  23.5 0.1 collective-permute-start
  23.5 1.3 %fusion.refs_0_ = s32[4]{0:T(128)} fusion(s32[1,4]{1,0:T(1,128)} %refs_0_.1, s32[]{:T(128)S(6)} %select_n.49), kind=kLoop, calls=%fused_computation.9 | loop fusion | flops 56 | bytes 36 | tf_op jit(solution)/shard_map/xor | solution.py:128
  24.8 0.2 collective-permute-done.refs_1_
  25.1 0.0 copy-done.5
  25.1 0.0 copy-start.10
  25.1 0.7 copy-done.10
  25.8 6.2 %shard_map.73.refs_2_ = bf16[256,1024]{1,0:T(8,128)(2,1)} custom-call(f32[256,256]{1,0:T(8,128)} %copy-done.5, f32[256,256]{1,0:T(8,128)} %copy-done.10, f32[256,1024]{1,0:T(8,128)} %refs_2_.3), custom_call_target="tpu_custom_call" | custom-call | flops 1006632960 | bytes 2097152 | tf_op jit(solution)/shard_map/pallas_call | solution.py:246
  31.9 0.0 copy-start
  31.9 2.2 %collective-permute-done.8.refs_5_ = bf16[256,1024]{1,0:T(8,128)(2,1)S(1)} collective-permute-done((bf16[256,1024]{1,0:T(8,128)(2,1)S(1)}, bf16[256,1024]{1,0:T(8,128)(2,1)S(1)}, u32[]{:S(2)}, u32[]{:S(2)}) %collective-permute-start.8) | collective-permute-done | bytes 524320 | tf_op jit(solution)/shard_map/ppermute | solution.py:119
  34.2 0.0 copy-start.8
  34.2 9.5 %collective-permute-done.7.refs_4_ = bf16[256,1024]{1,0:T(8,128)(2,1)S(1)} collective-permute-done((bf16[256,1024]{1,0:T(8,128)(2,1)S(1)}, bf16[256,1024]{1,0:T(8,128)(2,1)S(1)}, u32[]{:S(2)}, u32[]{:S(2)}) %collective-permute-start.7) | collective-permute-done | bytes 524320 | tf_op jit(solution)/shard_map/ppermute | solution.py:119
  43.6 0.0 copy-start.9
  43.6 0.0 collective-permute-done.6.refs_3_
  43.7 0.0 copy-done.8
  43.7 0.8 copy-done.9
  44.4 7.7 %shard_map.74 = (f32[4,1024,256]{2,1,0:T(8,128)}, bf16[4,256,1024]{2,1,0:T(8,128)(2,1)}) custom-call(s32[4]{0:T(128)} %fusion.refs_0_, f32[1024,1024]{1,0:T(8,128)} %refs_9_.1, bf16[256,1024]{1,0:T(8,128)(2,1)} %refs_2_.4, bf16[256,1024]{1,0:T(8,128)(2,1)} %collective-permute-done.6.refs_3_, bf16[256,1024]{1,0:T(8,128)(2,1)} %copy-done.9, ...), custom_call_target="tpu_custom_call" | custom-call | flops 2147483648 | bytes 12582912 | tf_op jit(solution)/shard_map/pallas_call | solution.py:266
  52.2 0.0 copy-start.6
  52.2 0.0 copy-start.7
  52.2 0.2 collective-permute-start.9
  52.4 0.0 copy-done
  52.4 0.0 collective-permute-start.1
  52.4 16.0 %collective-permute-done.1 = bf16[256,1024]{1,0:T(8,128)(2,1)S(1)} collective-permute-done((bf16[256,1024]{1,0:T(8,128)(2,1)S(1)}, bf16[256,1024]{1,0:T(8,128)(2,1)S(1)}, u32[]{:S(2)}, u32[]{:S(2)}) %collective-permute-start.1) | collective-permute-done | bytes 524320 | tf_op jit(solution)/shard_map/ppermute | solution.py:20
  68.4 0.1 broadcast_select_fusion.1
  68.5 1.8 %collective-permute-start.4 = (bf16[256,1024]{1,0:T(8,128)(2,1)S(1)}, bf16[256,1024]{1,0:T(8,128)(2,1)S(1)}, u32[]{:S(2)}, u32[]{:S(2)}) collective-permute-start(bf16[256,1024]{1,0:T(8,128)(2,1)S(1)} %get-tuple-element.30), channel_id=1, source_target_pairs={{0,6},{2,4},{4,2},{6,0},{8,14},{10,12},{12,10},{14,8},{16,22},{18,... | collective-permute-start | bytes 1572872 | tf_op jit(solution)/shard_map/ppermute | solution.py:119
  70.3 1.0 collective-permute-start.3
  71.3 0.8 collective-permute-start.2
  72.1 12.2 %collective-permute-done.4.refs_5_ = bf16[256,1024]{1,0:T(8,128)(2,1)S(1)} collective-permute-done((bf16[256,1024]{1,0:T(8,128)(2,1)S(1)}, bf16[256,1024]{1,0:T(8,128)(2,1)S(1)}, u32[]{:S(2)}, u32[]{:S(2)}) %collective-permute-start.4) | collective-permute-done | bytes 524320 | tf_op jit(solution)/shard_map/ppermute | solution.py:119
  84.3 0.0 copy-start.2
  84.3 9.8 %collective-permute-done.3.refs_4_ = bf16[256,1024]{1,0:T(8,128)(2,1)S(1)} collective-permute-done((bf16[256,1024]{1,0:T(8,128)(2,1)S(1)}, bf16[256,1024]{1,0:T(8,128)(2,1)S(1)}, u32[]{:S(2)}, u32[]{:S(2)}) %collective-permute-start.3) | collective-permute-done | bytes 524320 | tf_op jit(solution)/shard_map/ppermute | solution.py:119
  94.1 0.0 copy-start.3
  94.1 0.0 collective-permute-done.2.refs_3_
  94.1 0.0 copy-start.4
  94.1 0.0 copy-done.2
  94.1 0.8 copy-done.3
  94.9 0.2 copy-done.4
  95.1 4.3 %shard_map.75 = (bf16[6,256,256]{2,1,0:T(8,128)(2,1)}, bf16[4,256,1024]{2,1,0:T(8,128)(2,1)}) custom-call(s32[4]{0:T(128)} %fusion.refs_0_, bf16[4,256,1024]{2,1,0:T(8,128)(2,1)} %get-tuple-element.20.refs_1_, bf16[256,1024]{1,0:T(8,128)(2,1)} %shard_map.73.refs_2_, bf16[256,1024]{1,0:T(8,128)(2,1)} %copy-done.4, bf16[256,1024]{1,0:T(8,128)(2,1)} %copy-done.3, ...), custom_call_target="tpu_custom_call" | custom-call | tf_op jit(solution)/shard_map/pallas_call | solution.py:273
  99.4 0.0 collective-permute-start.10
  99.4 0.0 copy-done.6
  99.4 0.7 copy.8.refs_1_
  100.1 0.0 copy-done.7
  100.1 0.7 copy.9.refs_2_
  100.8 1.1 collective-permute-done.10.refs_7_
  101.9 0.0 copy-start.1
  101.9 0.0 collective-permute-done.9.refs_5_
  101.9 0.9 copy-done.1
  102.8 12.1 %shard_map.76 = f32[1024,1024]{1,0:T(8,128)} custom-call(s32[1,4]{1,0:T(1,128)} %refs_0_.1, s32[1,4,8,4]{3,2,1,0:T(8,128)} %copy.8.refs_1_, s32[1,4,8,4]{3,2,1,0:T(8,128)} %copy.9.refs_2_, f32[8]{0:T(128)} %refs_3_.1, f32[4,1024,256]{2,1,0:T(8,128)} %get-tuple-element.19.refs_4_, f32[4,1024,256]{2,1,0:T(8,128)} %collective-permute-done.9.refs_5_, ...), custom_call_target="tpu_custom_call" | custom-call | tf_op jit(solution)/shard_map/pallas_call | solution.py:283
Async XLA Ops:
  0.0 17.2 %collective-permute-start.5 = (bf16[256,1024]{1,0:T(8,128)(2,1)}, bf16[256,1024]{1,0:T(8,128)(2,1)S(1)}, u32[]{:S(2)}, u32[]{:S(2)}) collective-permute-start(bf16[256,1024]{1,0:T(8,128)(2,1)} %refs_2_.4), channel_id=1, source_target_pairs={{0,8},{2,10},{4,12},{6,14},{8,16},{10,18},{12,20},{14,22},{16,24},... | collective-permute-start | bytes 1572872 | tf_op jit(solution)/shard_map/ppermute | solution.py:20
  18.4 15.8 %collective-permute-start.8 = (bf16[256,1024]{1,0:T(8,128)(2,1)S(1)}, bf16[256,1024]{1,0:T(8,128)(2,1)S(1)}, u32[]{:S(2)}, u32[]{:S(2)}) collective-permute-start(bf16[256,1024]{1,0:T(8,128)(2,1)S(1)} %get-tuple-element.27), channel_id=1, source_target_pairs={{0,6},{2,4},{4,2},{6,0},{8,14},{10,12},{12,10},{14,8},{16,22},{18,... | collective-permute-start | bytes 1572872 | tf_op jit(solution)/shard_map/ppermute | solution.py:119
  20.9 22.8 %collective-permute-start.7 = (bf16[256,1024]{1,0:T(8,128)(2,1)S(1)}, bf16[256,1024]{1,0:T(8,128)(2,1)S(1)}, u32[]{:S(2)}, u32[]{:S(2)}) collective-permute-start(bf16[256,1024]{1,0:T(8,128)(2,1)S(1)} %get-tuple-element.28), channel_id=1, source_target_pairs={{0,4},{2,6},{4,0},{6,2},{8,12},{10,14},{12,8},{14,10},{16,20},{18,... | collective-permute-start | bytes 1572872 | tf_op jit(solution)/shard_map/ppermute | solution.py:119
  21.4 22.3 %collective-permute-start.6 = (bf16[256,1024]{1,0:T(8,128)(2,1)S(1)}, bf16[256,1024]{1,0:T(8,128)(2,1)}, u32[]{:S(2)}, u32[]{:S(2)}) collective-permute-start(bf16[256,1024]{1,0:T(8,128)(2,1)S(1)} %get-tuple-element.29), channel_id=1, source_target_pairs={{0,2},{2,0},{4,6},{6,4},{8,10},{10,8},{12,14},{14,12},{16,18},{18,... | collective-permute-start | bytes 1572872 | tf_op jit(solution)/shard_map/ppermute | solution.py:119
  23.5 1.6 %copy-start.5 = (f32[256,256]{1,0:T(8,128)}, f32[256,256]{1,0:T(8,128)S(1)}, u32[]{:S(2)}) copy-start(f32[256,256]{1,0:T(8,128)S(1)} %fusion.2.refs_0_) | copy-start | bytes 786436
  23.5 1.6 %collective-permute-start = (f32[256,256]{1,0:T(8,128)S(1)}, f32[256,256]{1,0:T(8,128)S(1)}, u32[]{:S(2)}, u32[]{:S(2)}) collective-permute-start(f32[256,256]{1,0:T(8,128)S(1)} %fusion.2.refs_0_), channel_id=1, source_target_pairs={{0,1},{1,0},{2,3},{3,2},{4,5},{5,4},{6,7},{7,6},{8,9},{9,8},{10,11... | collective-permute-start | bytes 786440 | tf_op jit(solution)/shard_map/ppermute | solution.py:20
  25.1 0.7 copy-start.10
  31.9 20.4 %copy-start = (bf16[256,1024]{1,0:T(8,128)(2,1)S(1)}, bf16[256,1024]{1,0:T(8,128)(2,1)}, u32[]{:S(2)}) copy-start(bf16[256,1024]{1,0:T(8,128)(2,1)} %shard_map.73.refs_2_) | copy-start | bytes 1572868
  34.2 9.5 %copy-start.8 = (bf16[256,1024]{1,0:T(8,128)(2,1)}, bf16[256,1024]{1,0:T(8,128)(2,1)S(1)}, u32[]{:S(2)}) copy-start(bf16[256,1024]{1,0:T(8,128)(2,1)S(1)} %collective-permute-done.8.refs_5_) | copy-start | bytes 1572868
  43.6 0.8 copy-start.9
  52.2 47.3 %copy-start.6 = (s32[1,4,8,4]{2,3,1,0:T(4,128)S(1)}, s32[1,4,8,4]{2,3,1,0:T(4,128)}, u32[]{:S(2)}) copy-start(s32[1,4,8,4]{2,3,1,0:T(4,128)} %param.10) | copy-start | bytes 1540
  52.2 47.9 %copy-start.7 = (s32[1,4,8,4]{2,3,1,0:T(4,128)S(1)}, s32[1,4,8,4]{2,3,1,0:T(4,128)}, u32[]{:S(2)}) copy-start(s32[1,4,8,4]{2,3,1,0:T(4,128)} %param.11) | copy-start | bytes 1540
  52.2 49.7 %collective-permute-start.9 = (f32[4,1024,256]{2,1,0:T(8,128)}, f32[4,1024,256]{2,1,0:T(8,128)}, u32[]{:S(2)}, u32[]{:S(2)}) collective-permute-start(f32[4,1024,256]{2,1,0:T(8,128)} %get-tuple-element.19.refs_4_), channel_id=1, source_target_pairs={{0,1},{1,0},{2,3},{3,2},{4,5},{5,4},{6,7},{7,6},{8,9},{9,8},{10,11... | collective-permute-start | bytes 12582920 | tf_op jit(solution)/shard_map/ppermute | solution.py:20
  52.4 16.0 %collective-permute-start.1 = (bf16[256,1024]{1,0:T(8,128)(2,1)S(1)}, bf16[256,1024]{1,0:T(8,128)(2,1)S(1)}, u32[]{:S(2)}, u32[]{:S(2)}) collective-permute-start(bf16[256,1024]{1,0:T(8,128)(2,1)S(1)} %copy-done), channel_id=1, source_target_pairs={{0,8},{2,10},{4,12},{6,14},{8,16},{10,18},{12,20},{14,22},{16,24},... | collective-permute-start | bytes 1572872 | tf_op jit(solution)/shard_map/ppermute | solution.py:20
  68.5 15.8 %collective-permute-start.4 = (bf16[256,1024]{1,0:T(8,128)(2,1)S(1)}, bf16[256,1024]{1,0:T(8,128)(2,1)S(1)}, u32[]{:S(2)}, u32[]{:S(2)}) collective-permute-start(bf16[256,1024]{1,0:T(8,128)(2,1)S(1)} %get-tuple-element.30), channel_id=1, source_target_pairs={{0,6},{2,4},{4,2},{6,0},{8,14},{10,12},{12,10},{14,8},{16,22},{18,... | collective-permute-start | bytes 1572872 | tf_op jit(solution)/shard_map/ppermute | solution.py:119
  70.3 23.8 %collective-permute-start.3 = (bf16[256,1024]{1,0:T(8,128)(2,1)S(1)}, bf16[256,1024]{1,0:T(8,128)(2,1)S(1)}, u32[]{:S(2)}, u32[]{:S(2)}) collective-permute-start(bf16[256,1024]{1,0:T(8,128)(2,1)S(1)} %get-tuple-element.31), channel_id=1, source_target_pairs={{0,4},{2,6},{4,0},{6,2},{8,12},{10,14},{12,8},{14,10},{16,20},{18,... | collective-permute-start | bytes 1572872 | tf_op jit(solution)/shard_map/ppermute | solution.py:119
  71.3 22.8 %collective-permute-start.2 = (bf16[256,1024]{1,0:T(8,128)(2,1)S(1)}, bf16[256,1024]{1,0:T(8,128)(2,1)S(1)}, u32[]{:S(2)}, u32[]{:S(2)}) collective-permute-start(bf16[256,1024]{1,0:T(8,128)(2,1)S(1)} %get-tuple-element.32), channel_id=1, source_target_pairs={{0,2},{2,0},{4,6},{6,4},{8,10},{10,8},{12,14},{14,12},{16,18},{18,... | collective-permute-start | bytes 1572872 | tf_op jit(solution)/shard_map/ppermute | solution.py:119
  84.3 9.8 %copy-start.2 = (bf16[256,1024]{1,0:T(8,128)(2,1)}, bf16[256,1024]{1,0:T(8,128)(2,1)S(1)}, u32[]{:S(2)}) copy-start(bf16[256,1024]{1,0:T(8,128)(2,1)S(1)} %collective-permute-done.4.refs_5_) | copy-start | bytes 1572868
  94.1 0.8 copy-start.3
  94.1 1.0 copy-start.4
  99.4 2.5 %collective-permute-start.10 = (bf16[6,256,256]{2,1,0:T(8,128)(2,1)}, bf16[6,256,256]{2,1,0:T(8,128)(2,1)S(1)}, u32[]{:S(2)}, u32[]{:S(2)}) collective-permute-start(bf16[6,256,256]{2,1,0:T(8,128)(2,1)} %get-tuple-element.25.refs_6_), channel_id=1, source_target_pairs={{0,1},{1,0},{2,3},{3,2},{4,5},{5,4},{6,7},{7,6},{8,9},{9,8},{10,11... | collective-permute-start | bytes 2359304 | tf_op jit(solution)/shard_map/ppermute | solution.py:20
  101.9 0.9 copy-start.1
